TPU v7x, 32 devices: a whole 2x2x4 slice. The times are simulated.
32 devices in a mesh: dp: 2 (over core), rows: 4 (over y, x), cols: 4 (over z).
Axes of the slice: x: 2, y: 2, z: 4, core: 2. Of those that a mesh axis runs over, the one named last changes fastest.
Arguments:
- tokens: bfloat16 [8192, 2048], P(('dp', 'rows', 'cols')), may hold values from -6 to 6
- attention_gain: float32 [2048], replicated, may hold values from 0.5 to 1.5
- mlp_gain: float32 [2048], replicated, may hold values from 0.5 to 1.5
- w_query: bfloat16 [2048, 2048], P('rows', 'cols'), may hold values from -0.25 to 0.25
- w_key: bfloat16 [2048, 256], P('rows'), may hold values from -0.125 to 0.125
- w_value: bfloat16 [2048, 256], P('rows'), may hold values from -0.125 to 0.125
- w_out: bfloat16 [2048, 2048], P(None, 'rows'), may hold values from -0.5 to 0.5
- w_gate: bfloat16 [2048, 5632], P('rows', 'cols'), may hold values from -0.125 to 0.125
- w_up: bfloat16 [2048, 5632], P('rows', 'cols'), may hold values from -0.125 to 0.125
- w_down: bfloat16 [5632, 2048], P('cols', 'rows'), may hold values from -0.078125 to 0.078125
- segment_ids: int32 [8, 1024], P(('dp', 'rows')), may hold values from 0 to 3, never falling along the last dimension, each value on 1 to 512 neighbouring positions
- skip_mask: int32 [8], P(('dp', 'rows')), may hold values 0 or 1
- cotangent: float32 [8192, 2048], P(('dp', 'rows', 'cols')), may hold values from -6 to 6
Outputs:
- output: bfloat16 [8192, 2048], P(('dp', 'rows', 'cols'))
- input_grad: float32 [8192, 2048], P(('dp', 'rows', 'cols'))
- attention_gain_grad: float32 [2048], replicated
- mlp_gain_grad: float32 [2048], replicated
- query_grad: float32 [2048, 2048], P(('dp', 'rows'), 'cols')
- key_grad: float32 [2048, 256], replicated
- value_grad: float32 [2048, 256], replicated
- out_grad: float32 [2048, 2048], P('cols', ('dp', 'rows'))
- gate_grad: float32 [2048, 5632], P(('dp', 'rows'), 'cols')
- up_grad: float32 [2048, 5632], P(('dp', 'rows'), 'cols')
- down_grad: float32 [5632, 2048], P('cols', ('dp', 'rows'))
Inputs may be any that keep to these rules, and one draw needn't show every extreme that they name: `segment_ids`: segment numbers never fall along a sequence of 1024 tokens; each sequence holds max(4, 4) documents, a document holds at most 512 tokens, and some document holds exactly that many.
All inputs are finite; a program needn't handle non-finite values. No bound on the sum of `skip_mask` on one device may be relied on, other than what follows from the above.
Results may differ from a plain program's by a relative error of at most 0.014.
Values may be sent and summed in bfloat16 or wider, within the bound.
No kernel may reach another device: no remote copies, remote signals or barrier semaphores. Data moves between devices by JAX's collectives and lax.ppermute only.
A program may use at most 320 MiB of HBM per device.

v0:
```python
import jax
import jax.numpy as jnp
from jax import lax
from jax.sharding import PartitionSpec as P

HEADS = 16
KV_HEADS = 2
HEAD_DIM = 128
epsilon = 1e-05
negative = -1e30
rope_base = 10000.0
bf16 = jnp.bfloat16
f32 = jnp.float32


def dot(left, right, dims):
    return lax.dot_general(
        left, right, ((dims[:1], dims[1:]), ((), ())), preferred_element_type=f32
    )


def nn(left, right):
    return dot(left, right, (1, 0))


def nt(left, right):
    return dot(left, right, (1, 1))


def tn(left, right):
    return dot(left, right, (0, 0))


def after(value, *earlier):
    return lax.optimization_barrier((value,) + earlier)[0]


def xor_blocks(blocks, index):
    bit = 1
    while bit < len(blocks):
        swap = index & bit != 0
        blocks = [jnp.where(swap, blocks[j ^ bit], blocks[j]) for j in range(len(blocks))]
        bit *= 2
    return blocks


def xor_order(value, index, count, axis):
    return jnp.concatenate(xor_blocks(jnp.split(value, count, axis), index), axis)


def rotary_tables(positions):
    half = HEAD_DIM // 2
    frequency = rope_base ** (-2.0 * jnp.arange(half, dtype=f32) / HEAD_DIM)
    angles = positions.astype(f32)[:, None] * frequency[None, :]
    return (jnp.cos(angles)[:, None, :], jnp.sin(angles)[:, None, :])


def rotate(values, cosine, sine, direction):
    heads = values.reshape(values.shape[0], -1, HEAD_DIM)
    half = HEAD_DIM // 2
    a, b = (heads[..., :half], heads[..., half:])
    s = sine * direction
    turned = jnp.concatenate([a * cosine - b * s, b * cosine + a * s], axis=-1)
    return turned.reshape(values.shape)


def norm_factor(values):
    return lax.rsqrt(jnp.mean(values * values, axis=-1, keepdims=True) + epsilon)


def norm_back(grad, values, factor, gain):
    y = grad * gain
    pulled = factor * y - values * factor**3 * jnp.mean(y * values, axis=-1, keepdims=True)
    return (pulled, jnp.sum(grad * values * factor, axis=0))


def local(
    tokens,
    attention_gain,
    mlp_gain,
    w_query,
    w_key,
    w_value,
    w_out,
    w_gate,
    w_up,
    w_down,
    segment_ids,
    skip_mask,
    cotangent,
):
    cols, rows = (lax.axis_size("cols"), lax.axis_size("rows"))
    c, r, d = (lax.axis_index("cols"), lax.axis_index("rows"), lax.axis_index("dp"))
    own, width = tokens.shape
    sequences, length = segment_ids.shape
    place = 2 * r + d
    blocks = 2 * rows
    step = width // blocks
    scale = HEAD_DIM ** (-0.5)

    def to_rows(value, a):
        return lax.ppermute(value, "rows", [(i, i ^ a) for i in range(rows)])

    def to_core(value):
        return lax.ppermute(value, "dp", [(0, 1), (1, 0)])

    def to_cols(value, k):
        return lax.ppermute(value, "cols", [(i, (i + k) % cols) for i in range(cols)])

    def along(value, k):
        return lax.ppermute(value, "cols", [(i, i + k) for i in range(cols) if 0 <= i + k < cols])

    def to_xor_cols(value, k):
        return lax.ppermute(value, "cols", [(i, i ^ k) for i in range(cols)])

    def fetch_rows(piece, first):
        if rows != 4:
            return [piece] + [to_rows(piece, a) for a in range(1, rows)]
        other = 3 - first
        near = to_rows(piece, first)
        far = to_rows(piece, other)
        both = to_rows(near, other)
        got = [piece, None, None, both]
        got[first], got[other] = (near, far)
        return got

    def with_core(got, own_other):
        pairs = []
        for j, piece in enumerate(got):
            pairs += [piece, own_other if j == 0 else to_core(piece)]
        return pairs

    def halves(weight, axis):
        low, high = jnp.split(weight, 2, axis)
        return (jnp.where(d == 0, low, high), jnp.where(d == 0, high, low))

    inputs = xor_order(tokens, place, blocks, 1).astype(f32)
    upstream = xor_order(cotangent, place, blocks, 1)
    gain_one = xor_order(attention_gain, place, blocks, 0)
    gain_two = xor_order(mlp_gain, place, blocks, 0)
    sequence = c * own // length
    start = c * own % length
    keep = (1 - lax.dynamic_index_in_dim(skip_mask, sequence, 0, False)).astype(f32)
    feed_own = (keep * upstream).astype(bf16)
    kv_mine, kv_other = halves(jnp.concatenate([w_key, w_value], 1), 0)
    kv_got = fetch_rows(kv_mine, 1)
    kv_matrix = jnp.concatenate(with_core(kv_got, kv_other), 0)
    q_mine, _ = halves(w_query, 0)
    q_parts = [q_mine] + [to_xor_cols(q_mine, k) for k in range(1, cols)]
    q_mine = jnp.concatenate(xor_blocks(q_parts, c), 1)
    q_lo, q_hi = jnp.split(q_mine, 2, 0)
    q_lo_got = fetch_rows(after(q_lo, kv_got[1]), 1)
    q_hi_got = fetch_rows(after(q_hi, kv_got[1]), 2)
    q_got = [jnp.concatenate([lo, hi], 0) for lo, hi in zip(q_lo_got, q_hi_got)]
    q_pairs = []
    for piece in q_got:
        q_pairs += [piece, to_core(piece)]
    q_matrix = jnp.concatenate(q_pairs, 0)
    o_mine, o_other = halves(w_out, 1)
    o_mine = after(o_mine, q_lo_got[1], q_hi_got[2])
    o_lo, o_hi = jnp.split(o_mine, 2, 0)
    o_lo_got, o_hi_got = (fetch_rows(o_lo, 1), fetch_rows(o_hi, 2))
    o_got = [jnp.concatenate([lo, hi], 0) for lo, hi in zip(o_lo_got, o_hi_got)]
    o_matrix = jnp.concatenate(with_core(o_got, o_other), 1)
    g_mine, g_other = halves(w_gate, 0)
    u_mine, u_other = halves(w_up, 0)
    g_got = fetch_rows(after(g_mine, o_lo_got[1], o_hi_got[2]), 1)
    u_got = fetch_rows(after(u_mine, o_lo_got[1], o_hi_got[2]), 2)
    g_matrix = jnp.concatenate(with_core(g_got, g_other), 0)
    u_matrix = jnp.concatenate(with_core(u_got, u_other), 0)
    w_mine, w_other = halves(w_down, 1)
    w_mine = after(w_mine, g_got[1], u_got[2])
    w_lo, w_hi = jnp.split(w_mine, 2, 0)
    w_lo_got, w_hi_got = (fetch_rows(w_lo, 1), fetch_rows(w_hi, 2))
    w_got = [jnp.concatenate([lo, hi], 0) for lo, hi in zip(w_lo_got, w_hi_got)]
    d_matrix = jnp.concatenate(with_core(w_got, w_other), 1)
    factor_one = norm_factor(inputs)
    normed = (inputs * factor_one * gain_one).astype(bf16)
    cosine, sine = rotary_tables(start + jnp.arange(own))
    kv_pre = nn(normed, kv_matrix)
    kv_width = KV_HEADS * HEAD_DIM
    kv_own = jnp.concatenate(
        [rotate(kv_pre[:, :kv_width], cosine, sine, 1.0), kv_pre[:, kv_width:]], 1
    ).astype(bf16)
    reach = min(-(-(length // 2 - 1) // own), length // own - 1)
    kv_before = [along(kv_own, k) for k in range(reach, 0, -1)]
    kv_all = jnp.concatenate(kv_before + [kv_own], 0)
    span = (reach + 1) * own
    q_rows = rotate(nn(normed, q_matrix), cosine, sine, 1.0).astype(bf16)
    feeds = [after(feed_own, q_parts[1])]
    for k in range(1, cols):
        feeds.append(to_cols(feeds[-1], 1))
    ids = lax.dynamic_index_in_dim(segment_ids, sequence, 0, False)
    ids_padded = jnp.concatenate([jnp.full((reach * own,), -1, ids.dtype), ids])
    ids_keys = lax.dynamic_slice_in_dim(ids_padded, start, span, 0)
    ids_rows = ids_keys[reach * own :]
    allowed = (ids_rows[:, None] == ids_keys[None, :]) & (
        (reach * own + jnp.arange(own))[:, None] >= jnp.arange(span)[None, :]
    )
    share = HEADS // KV_HEADS
    q_heads = q_rows.reshape(own, KV_HEADS, share, HEAD_DIM)
    k_heads = kv_all[:, :kv_width].reshape(span, KV_HEADS, HEAD_DIM)
    v_heads = kv_all[:, kv_width:].reshape(span, KV_HEADS, HEAD_DIM)

    def ein(form, a, b):
        return jnp.einsum(form, a, b, preferred_element_type=f32)

    scores = ein("bghe,kge->ghbk", q_heads, k_heads) * scale
    scores = jnp.where(allowed[None, None], scores, negative)
    top = jnp.max(scores, -1, keepdims=True)
    exponent = jnp.exp(scores - top)
    probs = exponent / jnp.sum(exponent, -1, keepdims=True)
    attend = probs.astype(bf16)
    mixed = ein("ghbk,kge->bghe", attend, v_heads).reshape(own, width).astype(bf16)
    branch = nn(mixed, o_matrix)
    middle = inputs + keep * branch
    factor_two = norm_factor(middle)
    hidden_own = (middle * factor_two * gain_two).astype(bf16)
    chunks = [hidden_own]
    for k in range(1, cols):
        chunks.append(to_cols(chunks[-1], 1))
    hiddens, gate_backs, up_backs, feed_parts, in_parts = ({}, {}, {}, {}, {})
    carry_in = None
    for k in list(range(1, cols)) + [0]:
        gate = nn(chunks[k], g_matrix)
        up = nn(chunks[k], u_matrix)
        back = nt(feeds[k], d_matrix)
        s = jax.nn.sigmoid(gate)
        hiddens[k] = (gate * s * up).astype(bf16)
        gate_backs[k] = (back * up * s * (1.0 + gate * (1.0 - s))).astype(bf16)
        up_backs[k] = (back * gate * s).astype(bf16)
        part = nt(gate_backs[k], g_matrix) + nt(up_backs[k], u_matrix)
        if carry_in is not None:
            part = part + carry_in.astype(f32)
        if k != 0:
            carry_in = to_cols(part.astype(bf16), 1)
        else:
            hidden_in_back = part
    order = list(range(cols))
    h_all = jnp.concatenate([chunks[k] for k in order], 0)
    f_all = jnp.concatenate([feeds[k] for k in order], 0)
    hid_all = jnp.concatenate([hiddens[k] for k in order], 0)
    gb_all = jnp.concatenate([gate_backs[k] for k in order], 0)
    ub_all = jnp.concatenate([up_backs[k] for k in order], 0)
    down_part = tn(hid_all, f_all).astype(bf16)
    gate_part = tn(h_all, gb_all).astype(bf16)
    up_part = tn(h_all, ub_all).astype(bf16)
    from_norm, mlp_gain_part = norm_back(hidden_in_back, middle, factor_two, gain_two)
    middle_grad = upstream + from_norm
    branch_back = (keep * middle_grad).astype(bf16)
    mixed_back = nt(branch_back, o_matrix).astype(bf16)
    out_part = tn(mixed, branch_back).astype(bf16)
    carry_out = None
    for k in list(range(1, cols)) + [0]:
        part = nn(after(hiddens[k], hidden_in_back), d_matrix)
        if carry_out is not None:
            part = part + carry_out.astype(f32)
        if k != 0:
            carry_out = to_cols(part.astype(bf16), 1)
    feed_values = part
    output = (middle + keep * feed_values).astype(bf16)
    mb_heads = mixed_back.reshape(own, KV_HEADS, share, HEAD_DIM)
    weight_back = ein("bghe,kge->ghbk", mb_heads, v_heads)
    inner = jnp.sum(weight_back * probs, -1, keepdims=True)
    score_back = (probs * (weight_back - inner)).astype(bf16)
    q_turned = ein("ghbk,kge->bghe", score_back, k_heads).reshape(own, width) * scale
    k_turned = ein("ghbk,bghe->kge", score_back, q_heads).reshape(span, kv_width) * scale
    v_turned = ein("ghbk,bghe->kge", attend, mb_heads).reshape(span, kv_width)
    kv_turned = jnp.concatenate([k_turned, v_turned], 1)
    kv_back_pre = kv_turned[reach * own :]
    for k in range(1, reach + 1):
        part = kv_turned[(reach - k) * own : (reach - k + 1) * own].astype(bf16)
        kv_back_pre = kv_back_pre + along(part, -k).astype(f32)
    q_back = rotate(q_turned, cosine, sine, -1.0).astype(bf16)
    kv_back = jnp.concatenate(
        [rotate(kv_back_pre[:, :kv_width], cosine, sine, -1.0), kv_back_pre[:, kv_width:]], 1
    ).astype(bf16)
    q_part = tn(normed, q_back).astype(bf16)
    normed_back = nt(q_back, q_matrix) + nt(kv_back, kv_matrix)
    from_norm, attention_gain_part = norm_back(normed_back, inputs, factor_one, gain_one)
    input_grad = xor_order(middle_grad + from_norm, place, blocks, 1)
    kv_part = tn(normed, kv_back).astype(bf16)

    def scatter(part, axis, first):
        parts = xor_blocks(jnp.split(part, blocks, axis), place ^ d * rows + r)
        keep_half = jnp.concatenate(parts[:rows], axis)
        send_half = jnp.concatenate(parts[rows:], axis)
        half = keep_half.astype(f32) + to_core(send_half).astype(f32)
        pieces = jnp.split(half, rows, axis)
        if rows != 4:
            total = pieces[0]
            for a in range(1, rows):
                total = total + to_rows(pieces[a].astype(bf16), a).astype(f32)
            return total
        other = 3 - first
        near = to_rows(jnp.concatenate([pieces[first], pieces[3]], axis).astype(bf16), first)
        near = jnp.split(near, 2, axis)
        mine = pieces[0] + near[0].astype(f32)
        theirs = pieces[other] + near[1].astype(f32)
        return mine + to_rows(theirs.astype(bf16), other).astype(f32)

    gate_grad = scatter(gate_part, 0, 1)
    up_grad = scatter(up_part, 0, 2)
    down_lo, down_hi = jnp.split(down_part, 2, 0)
    down_grad = jnp.concatenate([scatter(down_lo, 1, 1), scatter(down_hi, 1, 2)], 0)

    def scatter_cols(total, axis):
        pieces = xor_blocks(jnp.split(total.astype(bf16), cols, axis), c)
        result = pieces[0].astype(f32)
        for k in range(1, cols):
            result = result + to_xor_cols(pieces[k], k).astype(f32)
        return result

    out_lo, out_hi = jnp.split(out_part, 2, 0)
    out_sum = jnp.concatenate([scatter(out_lo, 1, 1), scatter(out_hi, 1, 2)], 0)
    out_grad = scatter_cols(out_sum, 0)
    q_lo, q_hi = jnp.split(q_part, 2, 1)
    q_sum = jnp.concatenate([scatter(q_lo, 0, 1), scatter(q_hi, 0, 2)], 1)
    query_grad = scatter_cols(q_sum, 1)
    kv_sum = scatter(kv_part, 0, 1).astype(bf16)
    total = kv_sum.astype(f32)
    for k in range(1, cols):
        total = total + to_xor_cols(kv_sum, k).astype(f32)
    total = total.astype(bf16)
    found = fetch_rows(total, 1)
    found = found + [to_core(x) for x in found]
    found = jnp.concatenate(xor_blocks(found, d * rows + r), 0).astype(f32)
    key_grad, value_grad = (found[:, :kv_width], found[:, kv_width:])
    gains = jnp.stack([attention_gain_part, mlp_gain_part])
    gains = lax.psum(xor_order(gains, place, blocks, 1), ("dp", "rows", "cols"))
    return (
        xor_order(output, place, blocks, 1),
        input_grad,
        gains[0],
        gains[1],
        query_grad,
        key_grad,
        value_grad,
        out_grad,
        gate_grad,
        up_grad,
        down_grad,
    )


def solution(mesh):
    return jax.shard_map(
        local,
        mesh=mesh,
        in_specs=(
            P(("dp", "rows", "cols"), None),
            P(),
            P(),
            P("rows", "cols"),
            P("rows", None),
            P("rows", None),
            P(None, "rows"),
            P("rows", "cols"),
            P("rows", "cols"),
            P("cols", "rows"),
            P(("dp", "rows"), None),
            P(("dp", "rows")),
            P(("dp", "rows", "cols"), None),
        ),
        out_specs=(
            P(("dp", "rows", "cols"), None),
            P(("dp", "rows", "cols"), None),
            P(),
            P(),
            P(("dp", "rows"), "cols"),
            P(),
            P(),
            P("cols", ("dp", "rows")),
            P(("dp", "rows"), "cols"),
            P(("dp", "rows"), "cols"),
            P("cols", ("dp", "rows")),
        ),
        check_vma=False,
    )
```

profile of v0, /device:TPU:0, one launch (start us, length us, event | category | flops | bytes accessed | tf_op | source)
XLA Modules:
  0.0 911.4 jit_solution(14802513030163577752)
XLA Ops:
  8.9 3.6 collective-permute-start.8
  25.5 9.0 collective-permute-done.9
  57.7 15.1 %collective-permute-done.16 = bf16[128,2048]{1,0:T(8,128)(2,1)} collective-permute-done((bf16[128,2048]{1,0:T(8,128)(2,1)}, bf16[128,2048]{1,0:T(8,128)(2,1)}, u32[]{:S(2)}, u32[]{:S(2)}) %collective-permute-start.16) | collective-permute-done | bytes 524320 | tf_op jit(solution)/shard_map/ppermute | solution.py:102
  98.6 3.8 collective-permute-done.22
  121.6 4.1 collective-permute-done.19
  135.2 5.5 collective-permute-done.27
  141.2 11.1 %collective-permute-done.28 = bf16[1024,256]{1,0:T(8,128)(2,1)S(1)} collective-permute-done((bf16[1024,256]{1,0:T(8,128)(2,1)}, bf16[1024,256]{1,0:T(8,128)(2,1)S(1)}, u32[]{:S(2)}, u32[]{:S(2)}) %collective-permute-start.28) | collective-permute-done | bytes 524320 | tf_op jit(solution)/shard_map/ppermute | solution.py:102
  157.3 9.7 %collective-permute-done.36 = bf16[256,1408]{1,0:T(8,128)(2,1)S(1)} collective-permute-done((bf16[256,1408]{1,0:T(8,128)(2,1)S(1)}, bf16[256,1408]{1,0:T(8,128)(2,1)S(1)}, u32[]{:S(2)}, u32[]{:S(2)}) %collective-permute-start.36) | collective-permute-done | bytes 720928 | tf_op jit(solution)/shard_map/ppermute | solution.py:102
  167.1 14.8 %collective-permute-start.52 = (bf16[256,2048]{1,0:T(8,128)(2,1)}, bf16[256,2048]{1,0:T(8,128)(2,1)}, u32[]{:S(2)}, u32[]{:S(2)}) collective-permute-start(bf16[256,2048]{1,0:T(8,128)(2,1)} %collective-permute-done.51), channel_id=1, source_target_pairs={{0,1},{1,2},{2,3},{3,0},{4,5},{5,6},{6,7},{7,4},{8,9},{9,10},{10,1... | collective-permute-start | bytes 3145736 | tf_op jit(solution)/shard_map/ppermute | solution.py:108
  186.3 5.7 convolution_bitcast_fusion
  195.0 10.4 %fusion.144 = (f32[2,8,256]{2,1,0:T(8,128)}, f32[2,8,256,768]{2,3,1,0:T(8,128)}) fusion(pred[256,768]{0,1:T(8,128)(4,1)} %fusion.85, bf16[768,2,128,1]{0,2,3,1:T(8,128)(2,1)S(1)} %copy-done.88, bf16[256,2,8,128]{3,0,2,1:T(8,128)(2,1)} %bitcast.160), kind=kOutput, calls=%fused_computation.794 | convolution fusion | flops 817890048 | bytes 14237696 | tf_op jit(solution)/shard_map/sub | solution.py:211
  205.5 8.6 fusion.121
  214.1 9.0 copy.51
  229.5 4.0 convolution_convert_fusion.8
  245.4 7.4 collective-permute-done.46
  269.2 13.0 %collective-permute-done.40 = bf16[256,1408]{1,0:T(8,128)(2,1)S(1)} collective-permute-done((bf16[256,1408]{1,0:T(8,128)(2,1)S(1)}, bf16[256,1408]{1,0:T(8,128)(2,1)S(1)}, u32[]{:S(2)}, u32[]{:S(2)}) %collective-permute-start.40) | collective-permute-done | bytes 720928 | tf_op jit(solution)/shard_map/ppermute | solution.py:102
  288.7 5.9 multiply_reduce_fusion.2
  296.6 4.1 fusion.146
  304.4 5.9 multiply_convert_fusion.13
  310.2 3.6 fusion.151
  323.8 4.6 fusion.155
  333.4 4.5 fusion.41
  338.0 13.6 %collective-permute-done.55 = bf16[256,2048]{1,0:T(8,128)(2,1)S(1)} collective-permute-done((bf16[256,2048]{1,0:T(8,128)(2,1)S(1)}, bf16[256,2048]{1,0:T(8,128)(2,1)S(1)}, u32[]{:S(2)}, u32[]{:S(2)}) %collective-permute-start.55) | collective-permute-done | bytes 1048608 | tf_op jit(solution)/shard_map/ppermute | solution.py:108
  351.6 4.8 fusion.152
  361.4 12.6 %collective-permute-done.57 = bf16[256,2048]{1,0:T(8,128)(2,1)S(1)} collective-permute-done((bf16[256,2048]{1,0:T(8,128)(2,1)S(1)}, bf16[256,2048]{1,0:T(8,128)(2,1)S(1)}, u32[]{:S(2)}, u32[]{:S(2)}) %collective-permute-start.57) | collective-permute-done | bytes 1048608 | tf_op jit(solution)/shard_map/ppermute | solution.py:108
  374.1 4.6 fusion.45
  379.1 17.4 %collective-permute-done.56 = bf16[256,2048]{1,0:T(8,128)(2,1)S(1)} collective-permute-done((bf16[256,2048]{1,0:T(8,128)(2,1)S(1)}, bf16[256,2048]{1,0:T(8,128)(2,1)S(1)}, u32[]{:S(2)}, u32[]{:S(2)}) %collective-permute-start.56) | collective-permute-done | bytes 1048608 | tf_op jit(solution)/shard_map/ppermute | solution.py:108
  396.6 4.8 fusion.149
  406.4 11.4 %collective-permute-done.58 = bf16[256,2048]{1,0:T(8,128)(2,1)S(1)} collective-permute-done((bf16[256,2048]{1,0:T(8,128)(2,1)S(1)}, bf16[256,2048]{1,0:T(8,128)(2,1)S(1)}, u32[]{:S(2)}, u32[]{:S(2)}) %collective-permute-start.58) | collective-permute-done | bytes 1048608 | tf_op jit(solution)/shard_map/ppermute | solution.py:108
  417.7 5.6 fusion.46
  423.4 8.3 convolution_convert_fusion.2
  436.1 5.9 pad_maximum_fusion.1
  442.0 8.3 convolution_convert_fusion.1
  454.5 6.2 pad_maximum_fusion.2
  461.2 8.1 convolution_convert_fusion
  477.8 5.6 multiply_reduce_fusion
  484.1 6.8 fusion.63
  492.0 5.9 fusion.1
  497.9 6.2 fusion.3
  508.0 3.7 copy.66
  517.5 7.2 fusion.66
  566.3 5.2 collective-permute-start.60
  587.5 37.9 %psum.7 = f32[2,2048]{1,0:T(2,128)S(1)} all-reduce(f32[2,2048]{1,0:T(2,128)S(1)} %constant_dynamic-update-slice_fusion.67), channel_id=1, replica_groups=mesh['dp'=2,'rows'=4,'cols'=4] {'dp','rows','cols'}, use_global_device_ids=true, to_apply=%region_9.10 | all-reduce | flops 4096 | bytes 32768 | tf_op jit(solution)/shard_map/psum | solution.py:330
  636.7 4.0 fusion.43
  640.7 9.6 %collective-permute-done.106 = bf16[704,512]{1,0:T(8,128)(2,1)S(1)} collective-permute-done((bf16[704,512]{1,0:T(8,128)(2,1)S(1)}, bf16[704,512]{1,0:T(8,128)(2,1)S(1)}, u32[]{:S(2)}, u32[]{:S(2)}) %collective-permute-start.106) | collective-permute-done | bytes 720928 | tf_op jit(solution)/shard_map/ppermute | solution.py:102
  656.7 7.0 collective-permute-done.107
  668.3 6.2 fusion.122
  675.8 6.6 convert_add_fusion
  682.6 5.8 collective-permute-done.75
  689.7 3.9 collective-permute-done.61
  695.0 5.7 fusion.42
  706.1 3.6 collective-permute-start.79
  720.2 18.8 %collective-permute-done.79 = bf16[256,512]{1,0:T(8,128)(2,1)} collective-permute-done((bf16[256,512]{1,0:T(8,128)(2,1)}, bf16[256,512]{1,0:T(8,128)(2,1)}, u32[]{:S(2)}, u32[]{:S(2)}) %collective-permute-start.79) | collective-permute-done | bytes 262176 | tf_op jit(solution)/shard_map/ppermute | solution.py:114
  740.4 12.2 %collective-permute-done.78 = bf16[256,512]{1,0:T(8,128)(2,1)S(1)} collective-permute-done((bf16[256,512]{1,0:T(8,128)(2,1)}, bf16[256,512]{1,0:T(8,128)(2,1)S(1)}, u32[]{:S(2)}, u32[]{:S(2)}) %collective-permute-start.78) | collective-permute-done | bytes 262176 | tf_op jit(solution)/shard_map/ppermute | solution.py:114
  757.5 4.8 fusion.44
  766.6 17.7 %collective-permute-done.88 = bf16[1024,512]{0,1:T(8,128)(2,1)S(1)} collective-permute-done((bf16[1024,512]{0,1:T(8,128)(2,1)}, bf16[1024,512]{0,1:T(8,128)(2,1)S(1)}, u32[]{:S(2)}, u32[]{:S(2)}) %collective-permute-start.88) | collective-permute-done | bytes 1048608 | tf_op jit(solution)/shard_map/ppermute | solution.py:102
  786.4 18.6 %collective-permute-done.80 = bf16[256,512]{1,0:T(8,128)(2,1)S(1)} collective-permute-done((bf16[256,512]{1,0:T(8,128)(2,1)S(1)}, bf16[256,512]{1,0:T(8,128)(2,1)S(1)}, u32[]{:S(2)}, u32[]{:S(2)}) %collective-permute-start.80) | collective-permute-done | bytes 262176 | tf_op jit(solution)/shard_map/ppermute | solution.py:102
  807.7 6.0 collective-permute-done.81
  825.2 23.8 %collective-permute-done.100 = bf16[512,1408]{1,0:T(8,128)(2,1)S(1)} collective-permute-done((bf16[512,1408]{1,0:T(8,128)(2,1)S(1)}, bf16[512,1408]{1,0:T(8,128)(2,1)S(1)}, u32[]{:S(2)}, u32[]{:S(2)}) %collective-permute-start.100) | collective-permute-done | bytes 1441824 | tf_op jit(solution)/shard_map/ppermute | solution.py:102
  852.1 8.1 collective-permute-done.70
  861.0 10.4 %collective-permute-done.92 = bf16[1024,256]{0,1:T(8,128)(2,1)S(1)} collective-permute-done((bf16[1024,256]{0,1:T(8,128)(2,1)S(1)}, bf16[1024,256]{0,1:T(8,128)(2,1)S(1)}, u32[]{:S(2)}, u32[]{:S(2)}) %collective-permute-start.92) | collective-permute-done | bytes 524320 | tf_op jit(solution)/shard_map/ppermute | solution.py:102
  873.0 17.0 %collective-permute-done.72 = bf16[256,512]{1,0:T(8,128)(2,1)S(1)} collective-permute-done((bf16[256,512]{1,0:T(8,128)(2,1)S(1)}, bf16[256,512]{1,0:T(8,128)(2,1)S(1)}, u32[]{:S(2)}, u32[]{:S(2)}) %collective-permute-start.72) | collective-permute-done | bytes 262176 | tf_op jit(solution)/shard_map/ppermute | solution.py:114
  890.0 5.2 collective-permute-start.93
  896.2 8.1 collective-permute-done.94
  (843 shorter events, 350.1 us)
Async XLA Ops:
  3.7 33.4 %collective-permute-start = (bf16[256,512]{1,0:T(8,128)(2,1)}, bf16[256,512]{1,0:T(8,128)(2,1)}, u32[]{:S(2)}, u32[]{:S(2)}) collective-permute-start(bf16[256,512]{1,0:T(8,128)(2,1)} %get-tuple-element.217), channel_id=1, source_target_pairs={{0,4},{4,0},{8,12},{12,8},{1,5},{5,1},{9,13},{13,9},{2,6},{6,2},{1... | collective-permute-start | bytes 786440 | tf_op jit(solution)/shard_map/ppermute | solution.py:102
  6.6 37.3 %collective-permute-start.2 = (bf16[256,512]{1,0:T(8,128)(2,1)}, bf16[256,512]{1,0:T(8,128)(2,1)}, u32[]{:S(2)}, u32[]{:S(2)}) collective-permute-start(bf16[256,512]{1,0:T(8,128)(2,1)} %get-tuple-element.217), channel_id=1, source_target_pairs={{0,8},{4,12},{8,0},{12,4},{1,9},{5,13},{9,1},{13,5},{2,10},{6,14},... | collective-permute-start | bytes 786440 | tf_op jit(solution)/shard_map/ppermute | solution.py:102
  12.5 22.1 %collective-permute-start.9 = (bf16[256,512]{1,0:T(8,128)(2,1)}, bf16[256,512]{1,0:T(8,128)(2,1)}, u32[]{:S(2)}, u32[]{:S(2)}) collective-permute-start(bf16[256,512]{1,0:T(8,128)(2,1)} %slice_select_fusion), channel_id=1, source_target_pairs={{0,2},{1,3},{2,0},{3,1},{4,6},{5,7},{6,4},{7,5},{8,10},{9,11},{10,... | collective-permute-start | bytes 786440 | tf_op jit(solution)/shard_map/ppermute | solution.py:114
  12.5 22.1 %collective-permute-start.10 = (bf16[256,512]{1,0:T(8,128)(2,1)}, bf16[256,512]{1,0:T(8,128)(2,1)}, u32[]{:S(2)}, u32[]{:S(2)}) collective-permute-start(bf16[256,512]{1,0:T(8,128)(2,1)} %slice_select_fusion), channel_id=1, source_target_pairs={{0,1},{1,0},{2,3},{3,2},{4,5},{5,4},{6,7},{7,6},{8,9},{9,8},{10,11... | collective-permute-start | bytes 786440 | tf_op jit(solution)/shard_map/ppermute | solution.py:114
  39.7 38.0 %collective-permute-start.13 = (bf16[128,2048]{1,0:T(8,128)(2,1)}, bf16[128,2048]{1,0:T(8,128)(2,1)}, u32[]{:S(2)}, u32[]{:S(2)}) collective-permute-start(bf16[128,2048]{1,0:T(8,128)(2,1)} %get-tuple-element.23), channel_id=1, source_target_pairs={{0,4},{4,0},{8,12},{12,8},{1,5},{5,1},{9,13},{13,9},{2,6},{6,2},{1... | collective-permute-start | bytes 1572872 | tf_op jit(solution)/shard_map/ppermute | solution.py:102
  47.1 33.4 %collective-permute-start.15 = (bf16[128,2048]{1,0:T(8,128)(2,1)}, bf16[128,2048]{1,0:T(8,128)(2,1)}, u32[]{:S(2)}, u32[]{:S(2)}) collective-permute-start(bf16[128,2048]{1,0:T(8,128)(2,1)} %get-tuple-element.22), channel_id=1, source_target_pairs={{0,8},{4,12},{8,0},{12,4},{1,9},{5,13},{9,1},{13,5},{2,10},{6,14},... | collective-permute-start | bytes 1572872 | tf_op jit(solution)/shard_map/ppermute | solution.py:102
  51.1 21.7 %collective-permute-start.16 = (bf16[128,2048]{1,0:T(8,128)(2,1)}, bf16[128,2048]{1,0:T(8,128)(2,1)}, u32[]{:S(2)}, u32[]{:S(2)}) collective-permute-start(bf16[128,2048]{1,0:T(8,128)(2,1)} %get-tuple-element.23), channel_id=1, source_target_pairs={{0,8},{4,12},{8,0},{12,4},{1,9},{5,13},{9,1},{13,5},{2,10},{6,14},... | collective-permute-start | bytes 1572872 | tf_op jit(solution)/shard_map/ppermute | solution.py:102
  51.7 52.9 %collective-permute-start.11 = (bf16[256,2048]{1,0:T(8,128)(2,1)}, bf16[256,2048]{1,0:T(8,128)(2,1)}, u32[]{:S(2)}, u32[]{:S(2)}) collective-permute-start(bf16[256,2048]{1,0:T(8,128)(2,1)} %pad_maximum_fusion.13), channel_id=1, source_target_pairs={{0,16},{16,0},{1,17},{17,1},{2,18},{18,2},{3,19},{19,3},{4,20},{20... | collective-permute-start | bytes 3145736 | tf_op jit(solution)/shard_map/ppermute | solution.py:105
  56.1 28.2 %collective-permute-start.7 = (bf16[256,512]{1,0:T(8,128)(2,1)S(1)}, bf16[256,512]{1,0:T(8,128)(2,1)S(1)}, u32[]{:S(2)}, u32[]{:S(2)}) collective-permute-start(bf16[256,512]{1,0:T(8,128)(2,1)S(1)} %pad_maximum_fusion.32), channel_id=1, source_target_pairs={{0,1},{1,2},{2,3},{4,5},{5,6},{6,7},{8,9},{9,10},{10,11},{12,13},{... | collective-permute-start | bytes 786440 | tf_op jit(solution)/shard_map/ppermute | solution.py:111
  84.3 72.8 %collective-permute-start.51 = (bf16[256,2048]{1,0:T(8,128)(2,1)}, bf16[256,2048]{1,0:T(8,128)(2,1)}, u32[]{:S(2)}, u32[]{:S(2)}) collective-permute-start(bf16[256,2048]{1,0:T(8,128)(2,1)} %multiply_convert_fusion.1), channel_id=1, source_target_pairs={{0,1},{1,2},{2,3},{3,0},{4,5},{5,6},{6,7},{7,4},{8,9},{9,10},{10,1... | collective-permute-start | bytes 3145736 | tf_op jit(solution)/shard_map/ppermute | solution.py:108
  96.5 29.8 %collective-permute-start.14 = (bf16[256,2048]{1,0:T(8,128)(2,1)}, bf16[256,2048]{1,0:T(8,128)(2,1)S(1)}, u32[]{:S(2)}, u32[]{:S(2)}) collective-permute-start(bf16[256,2048]{1,0:T(8,128)(2,1)} %pad_maximum_fusion.14), channel_id=1, source_target_pairs={{0,16},{16,0},{1,17},{17,1},{2,18},{18,2},{3,19},{19,3},{4,20},{20... | collective-permute-start | bytes 3145736 | tf_op jit(solution)/shard_map/ppermute | solution.py:105
  102.4 29.3 %collective-permute-start.17 = (bf16[256,2048]{1,0:T(8,128)(2,1)S(1)}, bf16[256,2048]{1,0:T(8,128)(2,1)S(1)}, u32[]{:S(2)}, u32[]{:S(2)}) collective-permute-start(bf16[256,2048]{1,0:T(8,128)(2,1)S(1)} %copy-done.114), channel_id=1, source_target_pairs={{0,16},{16,0},{1,17},{17,1},{2,18},{18,2},{3,19},{19,3},{4,20},{20... | collective-permute-start | bytes 3145736 | tf_op jit(solution)/shard_map/ppermute | solution.py:105
  120.1 34.6 %collective-permute-start.30 = (bf16[256,1408]{1,0:T(8,128)(2,1)}, bf16[256,1408]{1,0:T(8,128)(2,1)S(1)}, u32[]{:S(2)}, u32[]{:S(2)}) collective-permute-start(bf16[256,1408]{1,0:T(8,128)(2,1)} %get-tuple-element.25), channel_id=1, source_target_pairs={{0,4},{4,0},{8,12},{12,8},{1,5},{5,1},{9,13},{13,9},{2,6},{6,2},{1... | collective-permute-start | bytes 2162696 | tf_op jit(solution)/shard_map/ppermute | solution.py:102
  126.3 26.1 %collective-permute-start.28 = (bf16[1024,256]{1,0:T(8,128)(2,1)}, bf16[1024,256]{1,0:T(8,128)(2,1)S(1)}, u32[]{:S(2)}, u32[]{:S(2)}) collective-permute-start(bf16[1024,256]{1,0:T(8,128)(2,1)} %collective-permute-done.25), channel_id=1, source_target_pairs={{0,4},{4,0},{8,12},{12,8},{1,5},{5,1},{9,13},{13,9},{2,6},{6,2},{1... | collective-permute-start | bytes 1572872 | tf_op jit(solution)/shard_map/ppermute | solution.py:102
  131.7 23.0 %collective-permute-start.38 = (bf16[256,1408]{1,0:T(8,128)(2,1)S(1)}, bf16[256,1408]{1,0:T(8,128)(2,1)S(1)}, u32[]{:S(2)}, u32[]{:S(2)}) collective-permute-start(bf16[256,1408]{1,0:T(8,128)(2,1)S(1)} %copy-done.36), channel_id=1, source_target_pairs={{0,8},{4,12},{8,0},{12,4},{1,9},{5,13},{9,1},{13,5},{2,10},{6,14},... | collective-permute-start | bytes 2162696 | tf_op jit(solution)/shard_map/ppermute | solution.py:102
  140.7 26.4 %collective-permute-start.36 = (bf16[256,1408]{1,0:T(8,128)(2,1)S(1)}, bf16[256,1408]{1,0:T(8,128)(2,1)S(1)}, u32[]{:S(2)}, u32[]{:S(2)}) collective-permute-start(bf16[256,1408]{1,0:T(8,128)(2,1)S(1)} %copy-done.36), channel_id=1, source_target_pairs={{0,4},{4,0},{8,12},{12,8},{1,5},{5,1},{9,13},{13,9},{2,6},{6,2},{1... | collective-permute-start | bytes 2162696 | tf_op jit(solution)/shard_map/ppermute | solution.py:102
  152.3 105.4 %collective-permute-start.32 = (bf16[256,1408]{1,0:T(8,128)(2,1)}, bf16[256,1408]{1,0:T(8,128)(2,1)}, u32[]{:S(2)}, u32[]{:S(2)}) collective-permute-start(bf16[256,1408]{1,0:T(8,128)(2,1)} %get-tuple-element.25), channel_id=1, source_target_pairs={{0,8},{4,12},{8,0},{12,4},{1,9},{5,13},{9,1},{13,5},{2,10},{6,14},... | collective-permute-start | bytes 2162696 | tf_op jit(solution)/shard_map/ppermute | solution.py:102
  154.7 29.9 %collective-permute-start.20 = (bf16[256,2048]{1,0:T(8,128)(2,1)S(1)}, bf16[256,2048]{1,0:T(8,128)(2,1)S(1)}, u32[]{:S(2)}, u32[]{:S(2)}) collective-permute-start(bf16[256,2048]{1,0:T(8,128)(2,1)S(1)} %pad_maximum_fusion.16), channel_id=1, source_target_pairs={{0,16},{16,0},{1,17},{17,1},{2,18},{18,2},{3,19},{19,3},{4,20},{20... | collective-permute-start | bytes 3145736 | tf_op jit(solution)/shard_map/ppermute | solution.py:105
  154.7 68.4 %collective-permute-start.23 = (bf16[2048,256]{1,0:T(8,128)(2,1)}, bf16[2048,256]{1,0:T(8,128)(2,1)}, u32[]{:S(2)}, u32[]{:S(2)}) collective-permute-start(bf16[2048,256]{1,0:T(8,128)(2,1)} %pad_maximum_fusion.18), channel_id=1, source_target_pairs={{0,16},{16,0},{1,17},{17,1},{2,18},{18,2},{3,19},{19,3},{4,20},{20... | collective-permute-start | bytes 3145736 | tf_op jit(solution)/shard_map/ppermute | solution.py:105
  157.1 76.4 %collective-permute-start.26 = (bf16[2048,256]{1,0:T(8,128)(2,1)}, bf16[2048,256]{1,0:T(8,128)(2,1)}, u32[]{:S(2)}, u32[]{:S(2)}) collective-permute-start(bf16[2048,256]{1,0:T(8,128)(2,1)} %pad_maximum_fusion.19), channel_id=1, source_target_pairs={{0,16},{16,0},{1,17},{17,1},{2,18},{18,2},{3,19},{19,3},{4,20},{20... | collective-permute-start | bytes 3145736 | tf_op jit(solution)/shard_map/ppermute | solution.py:105
  167.1 100.5 %collective-permute-start.52 = (bf16[256,2048]{1,0:T(8,128)(2,1)}, bf16[256,2048]{1,0:T(8,128)(2,1)}, u32[]{:S(2)}, u32[]{:S(2)}) collective-permute-start(bf16[256,2048]{1,0:T(8,128)(2,1)} %collective-permute-done.51), channel_id=1, source_target_pairs={{0,1},{1,2},{2,3},{3,0},{4,5},{5,6},{6,7},{7,4},{8,9},{9,10},{10,1... | collective-permute-start | bytes 3145736 | tf_op jit(solution)/shard_map/ppermute | solution.py:108
  184.6 56.2 %collective-permute-start.42 = (bf16[704,256]{1,0:T(8,128)(2,1)}, bf16[704,256]{1,0:T(8,128)(2,1)}, u32[]{:S(2)}, u32[]{:S(2)}) collective-permute-start(bf16[704,256]{1,0:T(8,128)(2,1)} %get-tuple-element.388), channel_id=1, source_target_pairs={{0,4},{4,0},{8,12},{12,8},{1,5},{5,1},{9,13},{13,9},{2,6},{6,2},{1... | collective-permute-start | bytes 1081352 | tf_op jit(solution)/shard_map/ppermute | solution.py:102
  223.1 22.2 %collective-permute-start.45 = (bf16[704,256]{1,0:T(8,128)(2,1)}, bf16[704,256]{1,0:T(8,128)(2,1)S(1)}, u32[]{:S(2)}, u32[]{:S(2)}) collective-permute-start(bf16[704,256]{1,0:T(8,128)(2,1)} %get-tuple-element.388), channel_id=1, source_target_pairs={{0,8},{4,12},{8,0},{12,4},{1,9},{5,13},{9,1},{13,5},{2,10},{6,14},... | collective-permute-start | bytes 1081352 | tf_op jit(solution)/shard_map/ppermute | solution.py:102
  245.3 22.9 %collective-permute-start.39 = (bf16[256,1408]{1,0:T(8,128)(2,1)S(1)}, bf16[256,1408]{1,0:T(8,128)(2,1)S(1)}, u32[]{:S(2)}, u32[]{:S(2)}) collective-permute-start(bf16[256,1408]{1,0:T(8,128)(2,1)S(1)} %copy-done.118), channel_id=1, source_target_pairs={{0,16},{16,0},{1,17},{17,1},{2,18},{18,2},{3,19},{19,3},{4,20},{20... | collective-permute-start | bytes 2162696 | tf_op jit(solution)/shard_map/ppermute | solution.py:105
  257.7 24.5 %collective-permute-start.40 = (bf16[256,1408]{1,0:T(8,128)(2,1)S(1)}, bf16[256,1408]{1,0:T(8,128)(2,1)S(1)}, u32[]{:S(2)}, u32[]{:S(2)}) collective-permute-start(bf16[256,1408]{1,0:T(8,128)(2,1)S(1)} %copy-done.118), channel_id=1, source_target_pairs={{0,4},{4,0},{8,12},{12,8},{1,5},{5,1},{9,13},{13,9},{2,6},{6,2},{1... | collective-permute-start | bytes 2162696 | tf_op jit(solution)/shard_map/ppermute | solution.py:102
  264.0 23.1 %collective-permute-start.29 = (bf16[2048,256]{1,0:T(8,128)(2,1)S(1)}, bf16[2048,256]{1,0:T(8,128)(2,1)S(1)}, u32[]{:S(2)}, u32[]{:S(2)}) collective-permute-start(bf16[2048,256]{1,0:T(8,128)(2,1)S(1)} %copy-done.106), channel_id=1, source_target_pairs={{0,16},{16,0},{1,17},{17,1},{2,18},{18,2},{3,19},{19,3},{4,20},{20... | collective-permute-start | bytes 3145736 | tf_op jit(solution)/shard_map/ppermute | solution.py:105
  268.2 51.9 %collective-permute-start.53 = (bf16[256,2048]{1,0:T(8,128)(2,1)}, bf16[256,2048]{1,0:T(8,128)(2,1)S(1)}, u32[]{:S(2)}, u32[]{:S(2)}) collective-permute-start(bf16[256,2048]{1,0:T(8,128)(2,1)} %collective-permute-done.52), channel_id=1, source_target_pairs={{0,1},{1,2},{2,3},{3,0},{4,5},{5,6},{6,7},{7,4},{8,9},{9,10},{10,1... | collective-permute-start | bytes 3145736 | tf_op jit(solution)/shard_map/ppermute | solution.py:108
  295.8 27.8 %collective-permute-start.54 = (bf16[256,2048]{1,0:T(8,128)(2,1)S(1)}, bf16[256,2048]{1,0:T(8,128)(2,1)S(1)}, u32[]{:S(2)}, u32[]{:S(2)}) collective-permute-start(bf16[256,2048]{1,0:T(8,128)(2,1)S(1)} %multiply_convert_fusion.2), channel_id=1, source_target_pairs={{0,1},{1,2},{2,3},{3,0},{4,5},{5,6},{6,7},{7,4},{8,9},{9,10},{10,1... | collective-permute-start | bytes 3145736 | tf_op jit(solution)/shard_map/ppermute | solution.py:108
  323.6 28.0 %collective-permute-start.55 = (bf16[256,2048]{1,0:T(8,128)(2,1)S(1)}, bf16[256,2048]{1,0:T(8,128)(2,1)S(1)}, u32[]{:S(2)}, u32[]{:S(2)}) collective-permute-start(bf16[256,2048]{1,0:T(8,128)(2,1)S(1)} %collective-permute-done.54), channel_id=1, source_target_pairs={{0,1},{1,2},{2,3},{3,0},{4,5},{5,6},{6,7},{7,4},{8,9},{9,10},{10,1... | collective-permute-start | bytes 3145736 | tf_op jit(solution)/shard_map/ppermute | solution.py:108
  337.9 36.2 %collective-permute-start.57 = (bf16[256,2048]{1,0:T(8,128)(2,1)S(1)}, bf16[256,2048]{1,0:T(8,128)(2,1)S(1)}, u32[]{:S(2)}, u32[]{:S(2)}) collective-permute-start(bf16[256,2048]{1,0:T(8,128)(2,1)S(1)} %fusion.41), channel_id=1, source_target_pairs={{0,1},{1,2},{2,3},{3,0},{4,5},{5,6},{6,7},{7,4},{8,9},{9,10},{10,1... | collective-permute-start | bytes 3145736 | tf_op jit(solution)/shard_map/ppermute | solution.py:108
  351.6 44.9 %collective-permute-start.56 = (bf16[256,2048]{1,0:T(8,128)(2,1)S(1)}, bf16[256,2048]{1,0:T(8,128)(2,1)S(1)}, u32[]{:S(2)}, u32[]{:S(2)}) collective-permute-start(bf16[256,2048]{1,0:T(8,128)(2,1)S(1)} %collective-permute-done.55), channel_id=1, source_target_pairs={{0,1},{1,2},{2,3},{3,0},{4,5},{5,6},{6,7},{7,4},{8,9},{9,10},{10,1... | collective-permute-start | bytes 3145736 | tf_op jit(solution)/shard_map/ppermute | solution.py:108
  378.6 39.1 %collective-permute-start.58 = (bf16[256,2048]{1,0:T(8,128)(2,1)S(1)}, bf16[256,2048]{1,0:T(8,128)(2,1)S(1)}, u32[]{:S(2)}, u32[]{:S(2)}) collective-permute-start(bf16[256,2048]{1,0:T(8,128)(2,1)S(1)} %fusion.45), channel_id=1, source_target_pairs={{0,1},{1,2},{2,3},{3,0},{4,5},{5,6},{6,7},{7,4},{8,9},{9,10},{10,1... | collective-permute-start | bytes 3145736 | tf_op jit(solution)/shard_map/ppermute | solution.py:108
  423.4 54.4 %collective-permute-start.59 = (bf16[256,2048]{1,0:T(8,128)(2,1)}, bf16[256,2048]{1,0:T(8,128)(2,1)S(1)}, u32[]{:S(2)}, u32[]{:S(2)}) collective-permute-start(bf16[256,2048]{1,0:T(8,128)(2,1)} %fusion.46), channel_id=1, source_target_pairs={{0,1},{1,2},{2,3},{3,0},{4,5},{5,6},{6,7},{7,4},{8,9},{9,10},{10,1... | collective-permute-start | bytes 3145736 | tf_op jit(solution)/shard_map/ppermute | solution.py:108
  442.0 223.9 %collective-permute-start.96 = (bf16[1024,1408]{1,0:T(8,128)(2,1)}, bf16[1024,1408]{1,0:T(8,128)(2,1)}, u32[]{:S(2)}, u32[]{:S(2)}) collective-permute-start(bf16[1024,1408]{1,0:T(8,128)(2,1)} %pad_maximum_fusion.1), channel_id=1, source_target_pairs={{0,16},{16,0},{1,17},{17,1},{2,18},{18,2},{3,19},{19,3},{4,20},{20... | collective-permute-start | bytes 8650760 | tf_op jit(solution)/shard_map/ppermute | solution.py:105
  460.6 213.9 %collective-permute-start.99 = (bf16[1024,1408]{1,0:T(8,128)(2,1)}, bf16[1024,1408]{1,0:T(8,128)(2,1)}, u32[]{:S(2)}, u32[]{:S(2)}) collective-permute-start(bf16[1024,1408]{1,0:T(8,128)(2,1)} %pad_maximum_fusion.2), channel_id=1, source_target_pairs={{0,16},{16,0},{1,17},{17,1},{2,18},{18,2},{3,19},{19,3},{4,20},{20... | collective-permute-start | bytes 8650760 | tf_op jit(solution)/shard_map/ppermute | solution.py:105
  473.5 155.4 %collective-permute-start.105 = (bf16[704,1024]{1,0:T(8,128)(2,1)}, bf16[704,1024]{1,0:T(8,128)(2,1)}, u32[]{:S(2)}, u32[]{:S(2)}) collective-permute-start(bf16[704,1024]{1,0:T(8,128)(2,1)} %pad_maximum_fusion.10), channel_id=1, source_target_pairs={{0,16},{16,0},{1,17},{17,1},{2,18},{18,2},{3,19},{19,3},{4,20},{20... | collective-permute-start | bytes 4325384 | tf_op jit(solution)/shard_map/ppermute | solution.py:105
  565.8 65.3 %collective-permute-start.102 = (bf16[704,1024]{1,0:T(8,128)(2,1)}, bf16[704,1024]{1,0:T(8,128)(2,1)}, u32[]{:S(2)}, u32[]{:S(2)}) collective-permute-start(bf16[704,1024]{1,0:T(8,128)(2,1)} %pad_maximum_fusion.9), channel_id=1, source_target_pairs={{0,16},{16,0},{1,17},{17,1},{2,18},{18,2},{3,19},{19,3},{4,20},{20... | collective-permute-start | bytes 4325384 | tf_op jit(solution)/shard_map/ppermute | solution.py:105
  566.3 69.5 %collective-permute-start.60 = (bf16[256,2048]{1,0:T(8,128)(2,1)}, bf16[256,2048]{1,0:T(8,128)(2,1)}, u32[]{:S(2)}, u32[]{:S(2)}) collective-permute-start(bf16[256,2048]{1,0:T(8,128)(2,1)} %convolution_convert_fusion.7), channel_id=1, source_target_pairs={{0,1},{1,2},{2,3},{3,0},{4,5},{5,6},{6,7},{7,4},{8,9},{9,10},{10,1... | collective-permute-start | bytes 3145736 | tf_op jit(solution)/shard_map/ppermute | solution.py:108
  629.0 25.8 %collective-permute-start.74 = (bf16[1024,512]{1,0:T(8,128)(2,1)S(1)}, bf16[1024,512]{1,0:T(8,128)(2,1)S(1)}, u32[]{:S(2)}, u32[]{:S(2)}) collective-permute-start(bf16[1024,512]{1,0:T(8,128)(2,1)S(1)} %pad_maximum_fusion.23), channel_id=1, source_target_pairs={{0,16},{16,0},{1,17},{17,1},{2,18},{18,2},{3,19},{19,3},{4,20},{20... | collective-permute-start | bytes 3145736 | tf_op jit(solution)/shard_map/ppermute | solution.py:105
  650.3 50.4 %collective-permute-start.65 = (bf16[1024,1024]{1,0:T(8,128)(2,1)}, bf16[1024,1024]{1,0:T(8,128)(2,1)}, u32[]{:S(2)}, u32[]{:S(2)}) collective-permute-start(bf16[1024,1024]{1,0:T(8,128)(2,1)} %pad_maximum_fusion.3), channel_id=1, source_target_pairs={{0,16},{16,0},{1,17},{17,1},{2,18},{18,2},{3,19},{19,3},{4,20},{20... | collective-permute-start | bytes 6291464 | tf_op jit(solution)/shard_map/ppermute | solution.py:105
  663.7 49.7 %collective-permute-start.68 = (bf16[1024,1024]{1,0:T(8,128)(2,1)}, bf16[1024,1024]{1,0:T(8,128)(2,1)}, u32[]{:S(2)}, u32[]{:S(2)}) collective-permute-start(bf16[1024,1024]{1,0:T(8,128)(2,1)} %pad_maximum_fusion.4), channel_id=1, source_target_pairs={{0,16},{16,0},{1,17},{17,1},{2,18},{18,2},{3,19},{19,3},{4,20},{20... | collective-permute-start | bytes 6291464 | tf_op jit(solution)/shard_map/ppermute | solution.py:105
  664.3 41.9 %collective-permute-start.87 = (bf16[1024,1024]{0,1:T(8,128)(2,1)}, bf16[1024,1024]{0,1:T(8,128)(2,1)}, u32[]{:S(2)}, u32[]{:S(2)}) collective-permute-start(bf16[1024,1024]{0,1:T(8,128)(2,1)} %pad_maximum_fusion.5), channel_id=1, source_target_pairs={{0,16},{16,0},{1,17},{17,1},{2,18},{18,2},{3,19},{19,3},{4,20},{20... | collective-permute-start | bytes 6291464 | tf_op jit(solution)/shard_map/ppermute | solution.py:105
  665.9 27.8 %collective-permute-start.61 = (bf16[256,2048]{1,0:T(8,128)(2,1)}, bf16[256,2048]{1,0:T(8,128)(2,1)}, u32[]{:S(2)}, u32[]{:S(2)}) collective-permute-start(bf16[256,2048]{1,0:T(8,128)(2,1)} %fusion.43), channel_id=1, source_target_pairs={{0,1},{1,2},{2,3},{3,0},{4,5},{5,6},{6,7},{7,4},{8,9},{9,10},{10,1... | collective-permute-start | bytes 3145736 | tf_op jit(solution)/shard_map/ppermute | solution.py:108
  688.4 28.3 %collective-permute-start.90 = (bf16[1024,1024]{0,1:T(8,128)(2,1)}, bf16[1024,1024]{0,1:T(8,128)(2,1)S(1)}, u32[]{:S(2)}, u32[]{:S(2)}) collective-permute-start(bf16[1024,1024]{0,1:T(8,128)(2,1)} %pad_maximum_fusion.6), channel_id=1, source_target_pairs={{0,16},{16,0},{1,17},{17,1},{2,18},{18,2},{3,19},{19,3},{4,20},{20... | collective-permute-start | bytes 6291464 | tf_op jit(solution)/shard_map/ppermute | solution.py:105
  700.7 121.7 %collective-permute-start.97 = (bf16[512,1408]{1,0:T(8,128)(2,1)S(1)}, bf16[512,1408]{1,0:T(8,128)(2,1)}, u32[]{:S(2)}, u32[]{:S(2)}) collective-permute-start(bf16[512,1408]{1,0:T(8,128)(2,1)S(1)} %pad_maximum_fusion.8), channel_id=1, source_target_pairs={{0,4},{4,0},{8,12},{12,8},{1,5},{5,1},{9,13},{13,9},{2,6},{6,2},{1... | collective-permute-start | bytes 4325384 | tf_op jit(solution)/shard_map/ppermute | solution.py:102
  705.1 50.6 %collective-permute-start.62 = (bf16[256,2048]{1,0:T(8,128)(2,1)}, bf16[256,2048]{1,0:T(8,128)(2,1)}, u32[]{:S(2)}, u32[]{:S(2)}) collective-permute-start(bf16[256,2048]{1,0:T(8,128)(2,1)} %fusion.42), channel_id=1, source_target_pairs={{0,1},{1,2},{2,3},{3,0},{4,5},{5,6},{6,7},{7,4},{8,9},{9,10},{10,1... | collective-permute-start | bytes 3145736 | tf_op jit(solution)/shard_map/ppermute | solution.py:108
  706.1 32.9 %collective-permute-start.79 = (bf16[256,512]{1,0:T(8,128)(2,1)}, bf16[256,512]{1,0:T(8,128)(2,1)}, u32[]{:S(2)}, u32[]{:S(2)}) collective-permute-start(bf16[256,512]{1,0:T(8,128)(2,1)} %fusion.95), channel_id=1, source_target_pairs={{0,3},{1,2},{2,1},{3,0},{4,7},{5,6},{6,5},{7,4},{8,11},{9,10},{10,... | collective-permute-start | bytes 786440 | tf_op jit(solution)/shard_map/ppermute | solution.py:114
  713.5 39.2 %collective-permute-start.78 = (bf16[256,512]{1,0:T(8,128)(2,1)}, bf16[256,512]{1,0:T(8,128)(2,1)S(1)}, u32[]{:S(2)}, u32[]{:S(2)}) collective-permute-start(bf16[256,512]{1,0:T(8,128)(2,1)} %fusion.95), channel_id=1, source_target_pairs={{0,2},{1,3},{2,0},{3,1},{4,6},{5,7},{6,4},{7,5},{8,10},{9,11},{10,... | collective-permute-start | bytes 786440 | tf_op jit(solution)/shard_map/ppermute | solution.py:114
  716.7 37.5 %collective-permute-start.77 = (bf16[256,512]{1,0:T(8,128)(2,1)}, bf16[256,512]{1,0:T(8,128)(2,1)S(1)}, u32[]{:S(2)}, u32[]{:S(2)}) collective-permute-start(bf16[256,512]{1,0:T(8,128)(2,1)} %fusion.95), channel_id=1, source_target_pairs={{0,1},{1,0},{2,3},{3,2},{4,5},{5,4},{6,7},{7,6},{8,9},{9,8},{10,11... | collective-permute-start | bytes 786440 | tf_op jit(solution)/shard_map/ppermute | solution.py:114
  739.1 25.6 %collective-permute-start.66 = (bf16[512,1024]{1,0:T(8,128)(2,1)S(1)}, bf16[512,1024]{1,0:T(8,128)(2,1)S(1)}, u32[]{:S(2)}, u32[]{:S(2)}) collective-permute-start(bf16[512,1024]{1,0:T(8,128)(2,1)S(1)} %copy-done.113), channel_id=1, source_target_pairs={{0,8},{4,12},{8,0},{12,4},{1,9},{5,13},{9,1},{13,5},{2,10},{6,14},... | collective-permute-start | bytes 3145736 | tf_op jit(solution)/shard_map/ppermute | solution.py:102
  752.7 52.3 %collective-permute-start.69 = (bf16[512,1024]{1,0:T(8,128)(2,1)}, bf16[512,1024]{1,0:T(8,128)(2,1)S(1)}, u32[]{:S(2)}, u32[]{:S(2)}) collective-permute-start(bf16[512,1024]{1,0:T(8,128)(2,1)} %pad_maximum_fusion.22), channel_id=1, source_target_pairs={{0,4},{4,0},{8,12},{12,8},{1,5},{5,1},{9,13},{13,9},{2,6},{6,2},{1... | collective-permute-start | bytes 3145736 | tf_op jit(solution)/shard_map/ppermute | solution.py:102
  754.2 30.2 %collective-permute-start.88 = (bf16[1024,512]{0,1:T(8,128)(2,1)}, bf16[1024,512]{0,1:T(8,128)(2,1)S(1)}, u32[]{:S(2)}, u32[]{:S(2)}) collective-permute-start(bf16[1024,512]{0,1:T(8,128)(2,1)} %concatenate.300), channel_id=1, source_target_pairs={{0,8},{4,12},{8,0},{12,4},{1,9},{5,13},{9,1},{13,5},{2,10},{6,14},... | collective-permute-start | bytes 3145736 | tf_op jit(solution)/shard_map/ppermute | solution.py:102
  755.7 58.0 %collective-permute-start.91 = (bf16[1024,512]{0,1:T(8,128)(2,1)}, bf16[1024,512]{0,1:T(8,128)(2,1)S(1)}, u32[]{:S(2)}, u32[]{:S(2)}) collective-permute-start(bf16[1024,512]{0,1:T(8,128)(2,1)} %pad_maximum_fusion.24), channel_id=1, source_target_pairs={{0,4},{4,0},{8,12},{12,8},{1,5},{5,1},{9,13},{13,9},{2,6},{6,2},{1... | collective-permute-start | bytes 3145736 | tf_op jit(solution)/shard_map/ppermute | solution.py:102
  764.7 40.3 %collective-permute-start.80 = (bf16[256,512]{1,0:T(8,128)(2,1)S(1)}, bf16[256,512]{1,0:T(8,128)(2,1)S(1)}, u32[]{:S(2)}, u32[]{:S(2)}) collective-permute-start(bf16[256,512]{1,0:T(8,128)(2,1)S(1)} %add_convert_fusion.2), channel_id=1, source_target_pairs={{0,4},{4,0},{8,12},{12,8},{1,5},{5,1},{9,13},{13,9},{2,6},{6,2},{1... | collective-permute-start | bytes 786440 | tf_op jit(solution)/shard_map/ppermute | solution.py:102
  784.4 23.2 %collective-permute-start.83 = (bf16[256,512]{1,0:T(8,128)(2,1)S(1)}, bf16[256,512]{1,0:T(8,128)(2,1)S(1)}, u32[]{:S(2)}, u32[]{:S(2)}) collective-permute-start(bf16[256,512]{1,0:T(8,128)(2,1)S(1)} %add_convert_fusion.2), channel_id=1, source_target_pairs={{0,8},{4,12},{8,0},{12,4},{1,9},{5,13},{9,1},{13,5},{2,10},{6,14},... | collective-permute-start | bytes 786440 | tf_op jit(solution)/shard_map/ppermute | solution.py:102
  814.4 34.5 %collective-permute-start.100 = (bf16[512,1408]{1,0:T(8,128)(2,1)S(1)}, bf16[512,1408]{1,0:T(8,128)(2,1)S(1)}, u32[]{:S(2)}, u32[]{:S(2)}) collective-permute-start(bf16[512,1408]{1,0:T(8,128)(2,1)S(1)} %copy-done.98), channel_id=1, source_target_pairs={{0,8},{4,12},{8,0},{12,4},{1,9},{5,13},{9,1},{13,5},{2,10},{6,14},... | collective-permute-start | bytes 4325384 | tf_op jit(solution)/shard_map/ppermute | solution.py:102
  816.0 35.4 %collective-permute-start.67 = (bf16[256,1024]{1,0:T(8,128)(2,1)S(1)}, bf16[256,1024]{1,0:T(8,128)(2,1)S(1)}, u32[]{:S(2)}, u32[]{:S(2)}) collective-permute-start(bf16[256,1024]{1,0:T(8,128)(2,1)S(1)} %fusion.77), channel_id=1, source_target_pairs={{0,4},{4,0},{8,12},{12,8},{1,5},{5,1},{9,13},{13,9},{2,6},{6,2},{1... | collective-permute-start | bytes 1572872 | tf_op jit(solution)/shard_map/ppermute | solution.py:102
  816.4 43.8 %collective-permute-start.70 = (bf16[256,1024]{1,0:T(8,128)(2,1)}, bf16[256,1024]{1,0:T(8,128)(2,1)S(1)}, u32[]{:S(2)}, u32[]{:S(2)}) collective-permute-start(bf16[256,1024]{1,0:T(8,128)(2,1)} %fusion.74), channel_id=1, source_target_pairs={{0,8},{4,12},{8,0},{12,4},{1,9},{5,13},{9,1},{13,5},{2,10},{6,14},... | collective-permute-start | bytes 1572872 | tf_op jit(solution)/shard_map/ppermute | solution.py:102
  818.0 42.6 %collective-permute-start.89 = (bf16[1024,256]{0,1:T(8,128)(2,1)S(1)}, bf16[1024,256]{0,1:T(8,128)(2,1)S(1)}, u32[]{:S(2)}, u32[]{:S(2)}) collective-permute-start(bf16[1024,256]{0,1:T(8,128)(2,1)S(1)} %fusion.71), channel_id=1, source_target_pairs={{0,4},{4,0},{8,12},{12,8},{1,5},{5,1},{9,13},{13,9},{2,6},{6,2},{1... | collective-permute-start | bytes 1572872 | tf_op jit(solution)/shard_map/ppermute | solution.py:102
  822.4 49.0 %collective-permute-start.92 = (bf16[1024,256]{0,1:T(8,128)(2,1)S(1)}, bf16[1024,256]{0,1:T(8,128)(2,1)S(1)}, u32[]{:S(2)}, u32[]{:S(2)}) collective-permute-start(bf16[1024,256]{0,1:T(8,128)(2,1)S(1)} %fusion.68), channel_id=1, source_target_pairs={{0,8},{4,12},{8,0},{12,4},{1,9},{5,13},{9,1},{13,5},{2,10},{6,14},... | collective-permute-start | bytes 1572872 | tf_op jit(solution)/shard_map/ppermute | solution.py:102
  848.9 56.6 %collective-permute-start.98 = (bf16[256,1408]{1,0:T(8,128)(2,1)S(1)}, bf16[256,1408]{1,0:T(8,128)(2,1)S(1)}, u32[]{:S(2)}, u32[]{:S(2)}) collective-permute-start(bf16[256,1408]{1,0:T(8,128)(2,1)S(1)} %fusion.59), channel_id=1, source_target_pairs={{0,8},{4,12},{8,0},{12,4},{1,9},{5,13},{9,1},{13,5},{2,10},{6,14},... | collective-permute-start | bytes 2162696 | tf_op jit(solution)/shard_map/ppermute | solution.py:102
  851.5 56.9 %collective-permute-start.101 = (bf16[256,1408]{1,0:T(8,128)(2,1)}, bf16[256,1408]{1,0:T(8,128)(2,1)}, u32[]{:S(2)}, u32[]{:S(2)}) collective-permute-start(bf16[256,1408]{1,0:T(8,128)(2,1)} %fusion.57), channel_id=1, source_target_pairs={{0,4},{4,0},{8,12},{12,8},{1,5},{5,1},{9,13},{13,9},{2,6},{6,2},{1... | collective-permute-start | bytes 2162696 | tf_op jit(solution)/shard_map/ppermute | solution.py:102
  860.6 29.3 %collective-permute-start.72 = (bf16[256,512]{1,0:T(8,128)(2,1)S(1)}, bf16[256,512]{1,0:T(8,128)(2,1)S(1)}, u32[]{:S(2)}, u32[]{:S(2)}) collective-permute-start(bf16[256,512]{1,0:T(8,128)(2,1)S(1)} %get-tuple-element.371), channel_id=1, source_target_pairs={{0,2},{1,3},{2,0},{3,1},{4,6},{5,7},{6,4},{7,5},{8,10},{9,11},{10,... | collective-permute-start | bytes 786440 | tf_op jit(solution)/shard_map/ppermute | solution.py:114
  871.8 24.5 %collective-permute-start.95 = (bf16[512,256]{0,1:T(8,128)(2,1)S(1)}, bf16[512,256]{0,1:T(8,128)(2,1)S(1)}, u32[]{:S(2)}, u32[]{:S(2)}) collective-permute-start(bf16[512,256]{0,1:T(8,128)(2,1)S(1)} %get-tuple-element.361), channel_id=1, source_target_pairs={{0,3},{1,2},{2,1},{3,0},{4,7},{5,6},{6,5},{7,4},{8,11},{9,10},{10,... | collective-permute-start | bytes 786440 | tf_op jit(solution)/shard_map/ppermute | solution.py:114
  (223 other events, 3147.3 us)
where the time goes:
time: 922 us; the launch traced here: 911 us
  waiting for transfers between devices  318 us (34%)
  matrix products  175 us (19%)
  other arithmetic  159 us (17%)
  local copies, waits for them, and re-layouts  110 us (12%)
  starting transfers between devices  107 us (12%)
  blocking collectives  37.9 us (4%)
    ppermute x48, waiting for transfers between devices, to_rows(): return lax.ppermute(value, 'rows', [(i, i ^ a) for i in range(rows)])  192 us
    dot_general x36, matrix products, dot(): lax.dot_general(left, right, ((dims[:1], dims[1:]), ((), ())), preferred_...  150 us
    unnamed x413, local copies, waits for them, and re-layouts  75.2 us
    ppermute x12, waiting for transfers between devices, to_xor_cols(): return lax.ppermute(value, 'cols', [(i, i ^ k) for i in range(cols)])  65.2 us
    ppermute x12, waiting for transfers between devices, to_cols(): lax.ppermute(value, 'cols', [(i, (i + k) % cols) for i in range(cols)])  60.6 us
    ppermute x48, starting transfers between devices, to_rows(): return lax.ppermute(value, 'rows', [(i, i ^ a) for i in range(rows)])  55 us
    psum x1, blocking collectives, local(): gains = lax.psum(xor_order(gains, place, blocks, 1), ('dp', 'rows', 'cols'))  37.9 us
    select_n x30, other arithmetic, xor_blocks(): jnp.where(swap, blocks[j ^ bit], blocks[j])  34.6 us
  transfers between devices with their start and end apart: 108, of which 36 were waited for; matrix products, arithmetic and copies ran while one was open for 46% of the time, Pallas kernels for 0%

commit v1 on v0

--- a/solution.py
+++ b/solution.py
@@ -327,7 +327,8 @@
     found = jnp.concatenate(xor_blocks(found, d * rows + r), 0).astype(f32)
     key_grad, value_grad = (found[:, :kv_width], found[:, kv_width:])
     gains = jnp.stack([attention_gain_part, mlp_gain_part])
-    gains = lax.psum(xor_order(gains, place, blocks, 1), ("dp", "rows", "cols"))
+    array_here = xor_order(gains, place, blocks, 1)
+    gains = jnp.sum(lax.all_gather(array_here, ("dp", "rows", "cols")), 0)
     return (
         xor_order(output, place, blocks, 1),
         input_grad,

time: 922 us -> 964 us (1.046)
  blocking collectives: 37.9 us -> 77.4 us
    all_gather x0 -> x1, blocking collectives: none -> 77.4 us  [local(): gains = jnp.sum(lax.all_gather(array_here, ('dp', 'rows', 'cols')), 0)]
    psum x1 -> x0, blocking collectives: 37.9 us -> none  [local(): gains = lax.psum(xor_order(gains, place, blocks, 1), ('dp', 'rows', 'cols'))]
    unnamed x413 -> x421, local copies, waits for them, and re-layouts: 75.2 us -> 73.3 us
  transfers between devices with their start and end apart: 108 -> 108, of which waited for: 36 -> 37; matrix products, arithmetic and copies ran while one was open for 46% -> 44% of each run, Pallas kernels for 0% -> 0%
where the time goes in v1:
time: 964 us; the launch traced here: 954 us
  waiting for transfers between devices  321 us (33%)
  matrix products  175 us (18%)
  other arithmetic  163 us (17%)
  starting transfers between devices  107 us (11%)
  local copies, waits for them, and re-layouts  106 us (11%)
  blocking collectives  77.4 us (8%)
    ppermute x48, waiting for transfers between devices, to_rows(): return lax.ppermute(value, 'rows', [(i, i ^ a) for i in range(rows)])  195 us
    dot_general x36, matrix products, dot(): lax.dot_general(left, right, ((dims[:1], dims[1:]), ((), ())), preferred_...  151 us
    all_gather x1, blocking collectives, local(): gains = jnp.sum(lax.all_gather(array_here, ('dp', 'rows', 'cols')), 0)  77.4 us
    unnamed x421, local copies, waits for them, and re-layouts  73.3 us
    ppermute x12, waiting for transfers between devices, to_cols(): lax.ppermute(value, 'cols', [(i, (i + k) % cols) for i in range(cols)])  63.4 us
    ppermute x12, waiting for transfers between devices, to_xor_cols(): return lax.ppermute(value, 'cols', [(i, i ^ k) for i in range(cols)])  62.2 us
    ppermute x48, starting transfers between devices, to_rows(): return lax.ppermute(value, 'rows', [(i, i ^ a) for i in range(rows)])  56 us
    select_n x30, other arithmetic, xor_blocks(): jnp.where(swap, blocks[j ^ bit], blocks[j])  34.5 us
  transfers between devices with their start and end apart: 108, of which 37 were waited for; matrix products, arithmetic and copies ran while one was open for 44% of the time, Pallas kernels for 0%

profile of v1, /device:TPU:0, one launch (start us, length us, event | category | flops | bytes accessed | tf_op | source)
XLA Modules:
  0.0 953.6 jit_solution(8140685641167398144)
XLA Ops:
  28.2 6.3 collective-permute-done.9
  44.3 4.1 collective-permute-done.4
  58.5 12.0 %collective-permute-done.16 = bf16[128,2048]{1,0:T(8,128)(2,1)} collective-permute-done((bf16[128,2048]{1,0:T(8,128)(2,1)S(1)}, bf16[128,2048]{1,0:T(8,128)(2,1)}, u32[]{:S(2)}, u32[]{:S(2)}) %collective-permute-start.16) | collective-permute-done | bytes 524320 | tf_op jit(solution)/shard_map/ppermute | solution.py:102
  94.8 5.6 collective-permute-done.22
  117.7 4.9 collective-permute-done.19
  132.2 5.5 collective-permute-done.27
  138.2 11.1 %collective-permute-done.28 = bf16[1024,256]{1,0:T(8,128)(2,1)S(1)} collective-permute-done((bf16[1024,256]{1,0:T(8,128)(2,1)S(1)}, bf16[1024,256]{1,0:T(8,128)(2,1)S(1)}, u32[]{:S(2)}, u32[]{:S(2)}) %collective-permute-start.28) | collective-permute-done | bytes 524320 | tf_op jit(solution)/shard_map/ppermute | solution.py:102
  155.4 8.8 collective-permute-done.36
  164.2 14.9 %collective-permute-start.52 = (bf16[256,2048]{1,0:T(8,128)(2,1)}, bf16[256,2048]{1,0:T(8,128)(2,1)}, u32[]{:S(2)}, u32[]{:S(2)}) collective-permute-start(bf16[256,2048]{1,0:T(8,128)(2,1)} %collective-permute-done.51), channel_id=1, source_target_pairs={{0,1},{1,2},{2,3},{3,0},{4,5},{5,6},{6,7},{7,4},{8,9},{9,10},{10,1... | collective-permute-start | bytes 3145736 | tf_op jit(solution)/shard_map/ppermute | solution.py:108
  183.4 5.7 convolution_bitcast_fusion
  192.7 10.0 %fusion.144 = (f32[2,8,256]{2,1,0:T(8,128)S(1)}, f32[2,8,256,768]{2,3,1,0:T(8,128)}) fusion(pred[256,768]{0,1:T(8,128)(4,1)S(1)} %copy-done.134, bf16[768,2,128,1]{0,2,3,1:T(8,128)(2,1)S(1)} %copy-done.97, bf16[256,2,8,128]{3,0,2,1:T(8,128)(2,1)} %bitcast.161), kind=kOutput, calls=%fused_computation.794 | convolution fusion | flops 817890048 | bytes 14237696 | tf_op jit(solution)/shard_map/sub | solution.py:211
  202.7 8.4 fusion.121
  211.1 9.1 copy.68
  225.8 4.0 convolution_convert_fusion.8
  241.0 8.2 collective-permute-done.46
  265.5 12.3 %collective-permute-done.40 = bf16[256,1408]{1,0:T(8,128)(2,1)S(1)} collective-permute-done((bf16[256,1408]{1,0:T(8,128)(2,1)S(1)}, bf16[256,1408]{1,0:T(8,128)(2,1)S(1)}, u32[]{:S(2)}, u32[]{:S(2)}) %collective-permute-start.40) | collective-permute-done | bytes 720928 | tf_op jit(solution)/shard_map/ppermute | solution.py:102
  284.3 5.9 multiply_reduce_fusion.2
  292.2 4.1 fusion.146
  300.0 5.9 multiply_convert_fusion.13
  319.3 4.7 fusion.155
  329.1 4.5 fusion.41
  333.6 13.6 %collective-permute-done.55 = bf16[256,2048]{1,0:T(8,128)(2,1)S(1)} collective-permute-done((bf16[256,2048]{1,0:T(8,128)(2,1)S(1)}, bf16[256,2048]{1,0:T(8,128)(2,1)S(1)}, u32[]{:S(2)}, u32[]{:S(2)}) %collective-permute-start.55) | collective-permute-done | bytes 1048608 | tf_op jit(solution)/shard_map/ppermute | solution.py:108
  347.2 4.8 fusion.152
  357.1 12.6 %collective-permute-done.57 = bf16[256,2048]{1,0:T(8,128)(2,1)S(1)} collective-permute-done((bf16[256,2048]{1,0:T(8,128)(2,1)S(1)}, bf16[256,2048]{1,0:T(8,128)(2,1)S(1)}, u32[]{:S(2)}, u32[]{:S(2)}) %collective-permute-start.57) | collective-permute-done | bytes 1048608 | tf_op jit(solution)/shard_map/ppermute | solution.py:108
  369.7 4.5 fusion.45
  374.6 17.5 %collective-permute-done.56 = bf16[256,2048]{1,0:T(8,128)(2,1)S(1)} collective-permute-done((bf16[256,2048]{1,0:T(8,128)(2,1)S(1)}, bf16[256,2048]{1,0:T(8,128)(2,1)S(1)}, u32[]{:S(2)}, u32[]{:S(2)}) %collective-permute-start.56) | collective-permute-done | bytes 1048608 | tf_op jit(solution)/shard_map/ppermute | solution.py:108
  392.1 4.8 fusion.149
  402.1 11.2 %collective-permute-done.58 = bf16[256,2048]{1,0:T(8,128)(2,1)S(1)} collective-permute-done((bf16[256,2048]{1,0:T(8,128)(2,1)S(1)}, bf16[256,2048]{1,0:T(8,128)(2,1)S(1)}, u32[]{:S(2)}, u32[]{:S(2)}) %collective-permute-start.58) | collective-permute-done | bytes 1048608 | tf_op jit(solution)/shard_map/ppermute | solution.py:108
  413.3 5.5 fusion.46
  418.8 8.8 convolution_convert_fusion.2
  431.9 5.9 pad_maximum_fusion.1
  437.8 9.2 convolution_convert_fusion.1
  451.1 6.1 pad_maximum_fusion.2
  457.8 8.7 convolution_convert_fusion
  474.8 5.5 multiply_reduce_fusion
  481.0 6.8 fusion.63
  488.9 6.0 fusion.1
  495.0 6.2 fusion.3
  505.1 3.7 copy.83
  514.6 7.2 fusion.66
  563.4 5.2 collective-permute-start.60
  584.6 77.4 %all-gather.1 = f32[32,2,2048]{2,1,0:T(2,128)} all-gather(f32[1,2,2048]{2,1,0:T(2,128)S(1)} %bitcast.176), channel_id=2, replica_groups=mesh['dp'=2,'rows'=4,'cols'=4] {'dp','rows','cols'}, dimensions={0}, use_global_device_ids=true | all-gather | bytes 540672 | tf_op jit(solution)/shard_map/all_gather | solution.py:331
  669.0 8.6 collective-permute-start.106
  680.8 4.1 fusion.43
  684.9 9.5 collective-permute-done.106
  699.5 8.4 collective-permute-done.107
  710.4 6.2 fusion.122
  717.9 6.6 convert_add_fusion
  726.0 4.9 collective-permute-done.75
  732.3 5.5 collective-permute-done.61
  738.3 5.7 fusion.42
  749.4 3.9 collective-permute-start.79
  763.9 19.2 %collective-permute-done.79 = bf16[256,512]{1,0:T(8,128)(2,1)S(1)} collective-permute-done((bf16[256,512]{1,0:T(8,128)(2,1)S(1)}, bf16[256,512]{1,0:T(8,128)(2,1)S(1)}, u32[]{:S(2)}, u32[]{:S(2)}) %collective-permute-start.79) | collective-permute-done | bytes 262176 | tf_op jit(solution)/shard_map/ppermute | solution.py:114
  784.5 9.8 %collective-permute-done.78 = bf16[256,512]{1,0:T(8,128)(2,1)S(1)} collective-permute-done((bf16[256,512]{1,0:T(8,128)(2,1)S(1)}, bf16[256,512]{1,0:T(8,128)(2,1)S(1)}, u32[]{:S(2)}, u32[]{:S(2)}) %collective-permute-start.78) | collective-permute-done | bytes 262176 | tf_op jit(solution)/shard_map/ppermute | solution.py:114
  798.0 4.9 fusion.44
  803.7 5.5 collective-permute-done.66
  810.7 18.3 %collective-permute-done.88 = bf16[1024,512]{0,1:T(8,128)(2,1)S(1)} collective-permute-done((bf16[1024,512]{0,1:T(8,128)(2,1)}, bf16[1024,512]{0,1:T(8,128)(2,1)S(1)}, u32[]{:S(2)}, u32[]{:S(2)}) %collective-permute-start.88) | collective-permute-done | bytes 1048608 | tf_op jit(solution)/shard_map/ppermute | solution.py:102
  830.4 15.3 %collective-permute-done.80 = bf16[256,512]{1,0:T(8,128)(2,1)S(1)} collective-permute-done((bf16[256,512]{1,0:T(8,128)(2,1)S(1)}, bf16[256,512]{1,0:T(8,128)(2,1)S(1)}, u32[]{:S(2)}, u32[]{:S(2)}) %collective-permute-start.80) | collective-permute-done | bytes 262176 | tf_op jit(solution)/shard_map/ppermute | solution.py:102
  848.4 6.2 collective-permute-done.81
  866.6 23.9 %collective-permute-done.100 = bf16[512,1408]{1,0:T(8,128)(2,1)S(1)} collective-permute-done((bf16[512,1408]{1,0:T(8,128)(2,1)S(1)}, bf16[512,1408]{1,0:T(8,128)(2,1)S(1)}, u32[]{:S(2)}, u32[]{:S(2)}) %collective-permute-start.100) | collective-permute-done | bytes 1441824 | tf_op jit(solution)/shard_map/ppermute | solution.py:102
  893.6 8.2 collective-permute-done.70
  904.0 8.9 collective-permute-done.92
  915.0 19.1 %collective-permute-done.72 = bf16[256,512]{1,0:T(8,128)(2,1)S(1)} collective-permute-done((bf16[256,512]{1,0:T(8,128)(2,1)S(1)}, bf16[256,512]{1,0:T(8,128)(2,1)S(1)}, u32[]{:S(2)}, u32[]{:S(2)}) %collective-permute-start.72) | collective-permute-done | bytes 262176 | tf_op jit(solution)/shard_map/ppermute | solution.py:114
  938.5 7.7 collective-permute-done.94
  (852 shorter events, 351.7 us)
Async XLA Ops:
  3.7 32.4 %collective-permute-start = (bf16[256,512]{1,0:T(8,128)(2,1)}, bf16[256,512]{1,0:T(8,128)(2,1)}, u32[]{:S(2)}, u32[]{:S(2)}) collective-permute-start(bf16[256,512]{1,0:T(8,128)(2,1)} %get-tuple-element.228), channel_id=1, source_target_pairs={{0,4},{4,0},{8,12},{12,8},{1,5},{5,1},{9,13},{13,9},{2,6},{6,2},{1... | collective-permute-start | bytes 786440 | tf_op jit(solution)/shard_map/ppermute | solution.py:102
  6.6 34.0 %collective-permute-start.2 = (bf16[256,512]{1,0:T(8,128)(2,1)}, bf16[256,512]{1,0:T(8,128)(2,1)}, u32[]{:S(2)}, u32[]{:S(2)}) collective-permute-start(bf16[256,512]{1,0:T(8,128)(2,1)} %get-tuple-element.228), channel_id=1, source_target_pairs={{0,8},{4,12},{8,0},{12,4},{1,9},{5,13},{9,1},{13,5},{2,10},{6,14},... | collective-permute-start | bytes 786440 | tf_op jit(solution)/shard_map/ppermute | solution.py:102
  12.5 22.1 %collective-permute-start.9 = (bf16[256,512]{1,0:T(8,128)(2,1)}, bf16[256,512]{1,0:T(8,128)(2,1)}, u32[]{:S(2)}, u32[]{:S(2)}) collective-permute-start(bf16[256,512]{1,0:T(8,128)(2,1)} %slice_select_fusion), channel_id=1, source_target_pairs={{0,2},{1,3},{2,0},{3,1},{4,6},{5,7},{6,4},{7,5},{8,10},{9,11},{10,... | collective-permute-start | bytes 786440 | tf_op jit(solution)/shard_map/ppermute | solution.py:114
  12.5 22.1 %collective-permute-start.10 = (bf16[256,512]{1,0:T(8,128)(2,1)}, bf16[256,512]{1,0:T(8,128)(2,1)}, u32[]{:S(2)}, u32[]{:S(2)}) collective-permute-start(bf16[256,512]{1,0:T(8,128)(2,1)} %slice_select_fusion), channel_id=1, source_target_pairs={{0,1},{1,0},{2,3},{3,2},{4,5},{5,4},{6,7},{7,6},{8,9},{9,8},{10,11... | collective-permute-start | bytes 786440 | tf_op jit(solution)/shard_map/ppermute | solution.py:114
  37.5 37.9 %collective-permute-start.13 = (bf16[128,2048]{1,0:T(8,128)(2,1)S(1)}, bf16[128,2048]{1,0:T(8,128)(2,1)}, u32[]{:S(2)}, u32[]{:S(2)}) collective-permute-start(bf16[128,2048]{1,0:T(8,128)(2,1)S(1)} %get-tuple-element.23), channel_id=1, source_target_pairs={{0,4},{4,0},{8,12},{12,8},{1,5},{5,1},{9,13},{13,9},{2,6},{6,2},{1... | collective-permute-start | bytes 1572872 | tf_op jit(solution)/shard_map/ppermute | solution.py:102
  42.7 35.6 %collective-permute-start.15 = (bf16[128,2048]{1,0:T(8,128)(2,1)S(1)}, bf16[128,2048]{1,0:T(8,128)(2,1)}, u32[]{:S(2)}, u32[]{:S(2)}) collective-permute-start(bf16[128,2048]{1,0:T(8,128)(2,1)S(1)} %get-tuple-element.22), channel_id=1, source_target_pairs={{0,8},{4,12},{8,0},{12,4},{1,9},{5,13},{9,1},{13,5},{2,10},{6,14},... | collective-permute-start | bytes 1572872 | tf_op jit(solution)/shard_map/ppermute | solution.py:102
  49.3 21.2 %collective-permute-start.16 = (bf16[128,2048]{1,0:T(8,128)(2,1)S(1)}, bf16[128,2048]{1,0:T(8,128)(2,1)}, u32[]{:S(2)}, u32[]{:S(2)}) collective-permute-start(bf16[128,2048]{1,0:T(8,128)(2,1)S(1)} %get-tuple-element.23), channel_id=1, source_target_pairs={{0,8},{4,12},{8,0},{12,4},{1,9},{5,13},{9,1},{13,5},{2,10},{6,14},... | collective-permute-start | bytes 1572872 | tf_op jit(solution)/shard_map/ppermute | solution.py:102
  50.0 52.7 %collective-permute-start.11 = (bf16[256,2048]{1,0:T(8,128)(2,1)}, bf16[256,2048]{1,0:T(8,128)(2,1)}, u32[]{:S(2)}, u32[]{:S(2)}) collective-permute-start(bf16[256,2048]{1,0:T(8,128)(2,1)} %pad_maximum_fusion.13), channel_id=1, source_target_pairs={{0,16},{16,0},{1,17},{17,1},{2,18},{18,2},{3,19},{19,3},{4,20},{20... | collective-permute-start | bytes 3145736 | tf_op jit(solution)/shard_map/ppermute | solution.py:105
  57.0 24.1 %collective-permute-start.7 = (bf16[256,512]{1,0:T(8,128)(2,1)S(1)}, bf16[256,512]{1,0:T(8,128)(2,1)S(1)}, u32[]{:S(2)}, u32[]{:S(2)}) collective-permute-start(bf16[256,512]{1,0:T(8,128)(2,1)S(1)} %pad_maximum_fusion.32), channel_id=1, source_target_pairs={{0,1},{1,2},{2,3},{4,5},{5,6},{6,7},{8,9},{9,10},{10,11},{12,13},{... | collective-permute-start | bytes 786440 | tf_op jit(solution)/shard_map/ppermute | solution.py:111
  81.1 74.1 %collective-permute-start.51 = (bf16[256,2048]{1,0:T(8,128)(2,1)}, bf16[256,2048]{1,0:T(8,128)(2,1)}, u32[]{:S(2)}, u32[]{:S(2)}) collective-permute-start(bf16[256,2048]{1,0:T(8,128)(2,1)} %multiply_convert_fusion.1), channel_id=1, source_target_pairs={{0,1},{1,2},{2,3},{3,0},{4,5},{5,6},{6,7},{7,4},{8,9},{9,10},{10,1... | collective-permute-start | bytes 3145736 | tf_op jit(solution)/shard_map/ppermute | solution.py:108
  92.6 31.7 %collective-permute-start.14 = (bf16[256,2048]{1,0:T(8,128)(2,1)}, bf16[256,2048]{1,0:T(8,128)(2,1)S(1)}, u32[]{:S(2)}, u32[]{:S(2)}) collective-permute-start(bf16[256,2048]{1,0:T(8,128)(2,1)} %pad_maximum_fusion.14), channel_id=1, source_target_pairs={{0,16},{16,0},{1,17},{17,1},{2,18},{18,2},{3,19},{19,3},{4,20},{20... | collective-permute-start | bytes 3145736 | tf_op jit(solution)/shard_map/ppermute | solution.py:105
  100.4 29.4 %collective-permute-start.17 = (bf16[256,2048]{1,0:T(8,128)(2,1)S(1)}, bf16[256,2048]{1,0:T(8,128)(2,1)S(1)}, u32[]{:S(2)}, u32[]{:S(2)}) collective-permute-start(bf16[256,2048]{1,0:T(8,128)(2,1)S(1)} %copy-done.121), channel_id=1, source_target_pairs={{0,16},{16,0},{1,17},{17,1},{2,18},{18,2},{3,19},{19,3},{4,20},{20... | collective-permute-start | bytes 3145736 | tf_op jit(solution)/shard_map/ppermute | solution.py:105
  117.2 35.5 %collective-permute-start.30 = (bf16[256,1408]{1,0:T(8,128)(2,1)}, bf16[256,1408]{1,0:T(8,128)(2,1)S(1)}, u32[]{:S(2)}, u32[]{:S(2)}) collective-permute-start(bf16[256,1408]{1,0:T(8,128)(2,1)} %get-tuple-element.25), channel_id=1, source_target_pairs={{0,4},{4,0},{8,12},{12,8},{1,5},{5,1},{9,13},{13,9},{2,6},{6,2},{1... | collective-permute-start | bytes 2162696 | tf_op jit(solution)/shard_map/ppermute | solution.py:102
  124.3 25.0 %collective-permute-start.28 = (bf16[1024,256]{1,0:T(8,128)(2,1)S(1)}, bf16[1024,256]{1,0:T(8,128)(2,1)S(1)}, u32[]{:S(2)}, u32[]{:S(2)}) collective-permute-start(bf16[1024,256]{1,0:T(8,128)(2,1)S(1)} %collective-permute-done.25), channel_id=1, source_target_pairs={{0,4},{4,0},{8,12},{12,8},{1,5},{5,1},{9,13},{13,9},{2,6},{6,2},{1... | collective-permute-start | bytes 1572872 | tf_op jit(solution)/shard_map/ppermute | solution.py:102
  129.8 23.0 %collective-permute-start.38 = (bf16[256,1408]{1,0:T(8,128)(2,1)S(1)}, bf16[256,1408]{1,0:T(8,128)(2,1)S(1)}, u32[]{:S(2)}, u32[]{:S(2)}) collective-permute-start(bf16[256,1408]{1,0:T(8,128)(2,1)S(1)} %copy-done.43), channel_id=1, source_target_pairs={{0,8},{4,12},{8,0},{12,4},{1,9},{5,13},{9,1},{13,5},{2,10},{6,14},... | collective-permute-start | bytes 2162696 | tf_op jit(solution)/shard_map/ppermute | solution.py:102
  137.7 26.5 %collective-permute-start.36 = (bf16[256,1408]{1,0:T(8,128)(2,1)S(1)}, bf16[256,1408]{1,0:T(8,128)(2,1)S(1)}, u32[]{:S(2)}, u32[]{:S(2)}) collective-permute-start(bf16[256,1408]{1,0:T(8,128)(2,1)S(1)} %copy-done.43), channel_id=1, source_target_pairs={{0,4},{4,0},{8,12},{12,8},{1,5},{5,1},{9,13},{13,9},{2,6},{6,2},{1... | collective-permute-start | bytes 2162696 | tf_op jit(solution)/shard_map/ppermute | solution.py:102
  149.3 104.6 %collective-permute-start.32 = (bf16[256,1408]{1,0:T(8,128)(2,1)}, bf16[256,1408]{1,0:T(8,128)(2,1)}, u32[]{:S(2)}, u32[]{:S(2)}) collective-permute-start(bf16[256,1408]{1,0:T(8,128)(2,1)} %get-tuple-element.25), channel_id=1, source_target_pairs={{0,8},{4,12},{8,0},{12,4},{1,9},{5,13},{9,1},{13,5},{2,10},{6,14},... | collective-permute-start | bytes 2162696 | tf_op jit(solution)/shard_map/ppermute | solution.py:102
  152.8 29.0 %collective-permute-start.20 = (bf16[256,2048]{1,0:T(8,128)(2,1)S(1)}, bf16[256,2048]{1,0:T(8,128)(2,1)S(1)}, u32[]{:S(2)}, u32[]{:S(2)}) collective-permute-start(bf16[256,2048]{1,0:T(8,128)(2,1)S(1)} %pad_maximum_fusion.16), channel_id=1, source_target_pairs={{0,16},{16,0},{1,17},{17,1},{2,18},{18,2},{3,19},{19,3},{4,20},{20... | collective-permute-start | bytes 3145736 | tf_op jit(solution)/shard_map/ppermute | solution.py:105
  152.8 67.4 %collective-permute-start.23 = (bf16[2048,256]{1,0:T(8,128)(2,1)}, bf16[2048,256]{1,0:T(8,128)(2,1)}, u32[]{:S(2)}, u32[]{:S(2)}) collective-permute-start(bf16[2048,256]{1,0:T(8,128)(2,1)} %pad_maximum_fusion.18), channel_id=1, source_target_pairs={{0,16},{16,0},{1,17},{17,1},{2,18},{18,2},{3,19},{19,3},{4,20},{20... | collective-permute-start | bytes 3145736 | tf_op jit(solution)/shard_map/ppermute | solution.py:105
  155.2 74.7 %collective-permute-start.26 = (bf16[2048,256]{1,0:T(8,128)(2,1)}, bf16[2048,256]{1,0:T(8,128)(2,1)}, u32[]{:S(2)}, u32[]{:S(2)}) collective-permute-start(bf16[2048,256]{1,0:T(8,128)(2,1)} %pad_maximum_fusion.19), channel_id=1, source_target_pairs={{0,16},{16,0},{1,17},{17,1},{2,18},{18,2},{3,19},{19,3},{4,20},{20... | collective-permute-start | bytes 3145736 | tf_op jit(solution)/shard_map/ppermute | solution.py:105
  164.2 98.9 %collective-permute-start.52 = (bf16[256,2048]{1,0:T(8,128)(2,1)}, bf16[256,2048]{1,0:T(8,128)(2,1)}, u32[]{:S(2)}, u32[]{:S(2)}) collective-permute-start(bf16[256,2048]{1,0:T(8,128)(2,1)} %collective-permute-done.51), channel_id=1, source_target_pairs={{0,1},{1,2},{2,3},{3,0},{4,5},{5,6},{6,7},{7,4},{8,9},{9,10},{10,1... | collective-permute-start | bytes 3145736 | tf_op jit(solution)/shard_map/ppermute | solution.py:108
  181.8 55.4 %collective-permute-start.42 = (bf16[704,256]{1,0:T(8,128)(2,1)}, bf16[704,256]{1,0:T(8,128)(2,1)}, u32[]{:S(2)}, u32[]{:S(2)}) collective-permute-start(bf16[704,256]{1,0:T(8,128)(2,1)} %get-tuple-element.399), channel_id=1, source_target_pairs={{0,4},{4,0},{8,12},{12,8},{1,5},{5,1},{9,13},{13,9},{2,6},{6,2},{1... | collective-permute-start | bytes 1081352 | tf_op jit(solution)/shard_map/ppermute | solution.py:102
  240.9 23.7 %collective-permute-start.39 = (bf16[256,1408]{1,0:T(8,128)(2,1)S(1)}, bf16[256,1408]{1,0:T(8,128)(2,1)S(1)}, u32[]{:S(2)}, u32[]{:S(2)}) collective-permute-start(bf16[256,1408]{1,0:T(8,128)(2,1)S(1)} %copy-done.125), channel_id=1, source_target_pairs={{0,16},{16,0},{1,17},{17,1},{2,18},{18,2},{3,19},{19,3},{4,20},{20... | collective-permute-start | bytes 2162696 | tf_op jit(solution)/shard_map/ppermute | solution.py:105
  253.9 23.9 %collective-permute-start.40 = (bf16[256,1408]{1,0:T(8,128)(2,1)S(1)}, bf16[256,1408]{1,0:T(8,128)(2,1)S(1)}, u32[]{:S(2)}, u32[]{:S(2)}) collective-permute-start(bf16[256,1408]{1,0:T(8,128)(2,1)S(1)} %copy-done.125), channel_id=1, source_target_pairs={{0,4},{4,0},{8,12},{12,8},{1,5},{5,1},{9,13},{13,9},{2,6},{6,2},{1... | collective-permute-start | bytes 2162696 | tf_op jit(solution)/shard_map/ppermute | solution.py:102
  260.4 22.3 %collective-permute-start.29 = (bf16[2048,256]{1,0:T(8,128)(2,1)S(1)}, bf16[2048,256]{1,0:T(8,128)(2,1)S(1)}, u32[]{:S(2)}, u32[]{:S(2)}) collective-permute-start(bf16[2048,256]{1,0:T(8,128)(2,1)S(1)} %copy-done.119), channel_id=1, source_target_pairs={{0,16},{16,0},{1,17},{17,1},{2,18},{18,2},{3,19},{19,3},{4,20},{20... | collective-permute-start | bytes 3145736 | tf_op jit(solution)/shard_map/ppermute | solution.py:105
  264.6 49.6 %collective-permute-start.53 = (bf16[256,2048]{1,0:T(8,128)(2,1)}, bf16[256,2048]{1,0:T(8,128)(2,1)S(1)}, u32[]{:S(2)}, u32[]{:S(2)}) collective-permute-start(bf16[256,2048]{1,0:T(8,128)(2,1)} %collective-permute-done.52), channel_id=1, source_target_pairs={{0,1},{1,2},{2,3},{3,0},{4,5},{5,6},{6,7},{7,4},{8,9},{9,10},{10,1... | collective-permute-start | bytes 3145736 | tf_op jit(solution)/shard_map/ppermute | solution.py:108
  291.4 27.8 %collective-permute-start.54 = (bf16[256,2048]{1,0:T(8,128)(2,1)S(1)}, bf16[256,2048]{1,0:T(8,128)(2,1)S(1)}, u32[]{:S(2)}, u32[]{:S(2)}) collective-permute-start(bf16[256,2048]{1,0:T(8,128)(2,1)S(1)} %multiply_convert_fusion.2), channel_id=1, source_target_pairs={{0,1},{1,2},{2,3},{3,0},{4,5},{5,6},{6,7},{7,4},{8,9},{9,10},{10,1... | collective-permute-start | bytes 3145736 | tf_op jit(solution)/shard_map/ppermute | solution.py:108
  319.2 28.0 %collective-permute-start.55 = (bf16[256,2048]{1,0:T(8,128)(2,1)S(1)}, bf16[256,2048]{1,0:T(8,128)(2,1)S(1)}, u32[]{:S(2)}, u32[]{:S(2)}) collective-permute-start(bf16[256,2048]{1,0:T(8,128)(2,1)S(1)} %collective-permute-done.54), channel_id=1, source_target_pairs={{0,1},{1,2},{2,3},{3,0},{4,5},{5,6},{6,7},{7,4},{8,9},{9,10},{10,1... | collective-permute-start | bytes 3145736 | tf_op jit(solution)/shard_map/ppermute | solution.py:108
  333.5 36.1 %collective-permute-start.57 = (bf16[256,2048]{1,0:T(8,128)(2,1)S(1)}, bf16[256,2048]{1,0:T(8,128)(2,1)S(1)}, u32[]{:S(2)}, u32[]{:S(2)}) collective-permute-start(bf16[256,2048]{1,0:T(8,128)(2,1)S(1)} %fusion.41), channel_id=1, source_target_pairs={{0,1},{1,2},{2,3},{3,0},{4,5},{5,6},{6,7},{7,4},{8,9},{9,10},{10,1... | collective-permute-start | bytes 3145736 | tf_op jit(solution)/shard_map/ppermute | solution.py:108
  347.2 44.9 %collective-permute-start.56 = (bf16[256,2048]{1,0:T(8,128)(2,1)S(1)}, bf16[256,2048]{1,0:T(8,128)(2,1)S(1)}, u32[]{:S(2)}, u32[]{:S(2)}) collective-permute-start(bf16[256,2048]{1,0:T(8,128)(2,1)S(1)} %collective-permute-done.55), channel_id=1, source_target_pairs={{0,1},{1,2},{2,3},{3,0},{4,5},{5,6},{6,7},{7,4},{8,9},{9,10},{10,1... | collective-permute-start | bytes 3145736 | tf_op jit(solution)/shard_map/ppermute | solution.py:108
  374.2 39.1 %collective-permute-start.58 = (bf16[256,2048]{1,0:T(8,128)(2,1)S(1)}, bf16[256,2048]{1,0:T(8,128)(2,1)S(1)}, u32[]{:S(2)}, u32[]{:S(2)}) collective-permute-start(bf16[256,2048]{1,0:T(8,128)(2,1)S(1)} %fusion.45), channel_id=1, source_target_pairs={{0,1},{1,2},{2,3},{3,0},{4,5},{5,6},{6,7},{7,4},{8,9},{9,10},{10,1... | collective-permute-start | bytes 3145736 | tf_op jit(solution)/shard_map/ppermute | solution.py:108
  418.8 56.0 %collective-permute-start.59 = (bf16[256,2048]{1,0:T(8,128)(2,1)}, bf16[256,2048]{1,0:T(8,128)(2,1)S(1)}, u32[]{:S(2)}, u32[]{:S(2)}) collective-permute-start(bf16[256,2048]{1,0:T(8,128)(2,1)} %fusion.46), channel_id=1, source_target_pairs={{0,1},{1,2},{2,3},{3,0},{4,5},{5,6},{6,7},{7,4},{8,9},{9,10},{10,1... | collective-permute-start | bytes 3145736 | tf_op jit(solution)/shard_map/ppermute | solution.py:108
  437.8 272.2 %collective-permute-start.96 = (bf16[1024,1408]{1,0:T(8,128)(2,1)}, bf16[1024,1408]{1,0:T(8,128)(2,1)}, u32[]{:S(2)}, u32[]{:S(2)}) collective-permute-start(bf16[1024,1408]{1,0:T(8,128)(2,1)} %pad_maximum_fusion.1), channel_id=1, source_target_pairs={{0,16},{16,0},{1,17},{17,1},{2,18},{18,2},{3,19},{19,3},{4,20},{20... | collective-permute-start | bytes 8650760 | tf_op jit(solution)/shard_map/ppermute | solution.py:105
  457.2 259.5 %collective-permute-start.99 = (bf16[1024,1408]{1,0:T(8,128)(2,1)}, bf16[1024,1408]{1,0:T(8,128)(2,1)}, u32[]{:S(2)}, u32[]{:S(2)}) collective-permute-start(bf16[1024,1408]{1,0:T(8,128)(2,1)} %pad_maximum_fusion.2), channel_id=1, source_target_pairs={{0,16},{16,0},{1,17},{17,1},{2,18},{18,2},{3,19},{19,3},{4,20},{20... | collective-permute-start | bytes 8650760 | tf_op jit(solution)/shard_map/ppermute | solution.py:105
  470.7 196.2 %collective-permute-start.105 = (bf16[704,1024]{1,0:T(8,128)(2,1)}, bf16[704,1024]{1,0:T(8,128)(2,1)}, u32[]{:S(2)}, u32[]{:S(2)}) collective-permute-start(bf16[704,1024]{1,0:T(8,128)(2,1)} %pad_maximum_fusion.10), channel_id=1, source_target_pairs={{0,16},{16,0},{1,17},{17,1},{2,18},{18,2},{3,19},{19,3},{4,20},{20... | collective-permute-start | bytes 4325384 | tf_op jit(solution)/shard_map/ppermute | solution.py:105
  562.9 106.1 %collective-permute-start.102 = (bf16[704,1024]{1,0:T(8,128)(2,1)}, bf16[704,1024]{1,0:T(8,128)(2,1)}, u32[]{:S(2)}, u32[]{:S(2)}) collective-permute-start(bf16[704,1024]{1,0:T(8,128)(2,1)} %pad_maximum_fusion.9), channel_id=1, source_target_pairs={{0,16},{16,0},{1,17},{17,1},{2,18},{18,2},{3,19},{19,3},{4,20},{20... | collective-permute-start | bytes 4325384 | tf_op jit(solution)/shard_map/ppermute | solution.py:105
  563.4 116.5 %collective-permute-start.60 = (bf16[256,2048]{1,0:T(8,128)(2,1)}, bf16[256,2048]{1,0:T(8,128)(2,1)}, u32[]{:S(2)}, u32[]{:S(2)}) collective-permute-start(bf16[256,2048]{1,0:T(8,128)(2,1)} %convolution_convert_fusion.7), channel_id=1, source_target_pairs={{0,1},{1,2},{2,3},{3,0},{4,5},{5,6},{6,7},{7,4},{8,9},{9,10},{10,1... | collective-permute-start | bytes 3145736 | tf_op jit(solution)/shard_map/ppermute | solution.py:108
  666.8 31.7 %collective-permute-start.74 = (bf16[1024,512]{1,0:T(8,128)(2,1)S(1)}, bf16[1024,512]{1,0:T(8,128)(2,1)S(1)}, u32[]{:S(2)}, u32[]{:S(2)}) collective-permute-start(bf16[1024,512]{1,0:T(8,128)(2,1)S(1)} %pad_maximum_fusion.23), channel_id=1, source_target_pairs={{0,16},{16,0},{1,17},{17,1},{2,18},{18,2},{3,19},{19,3},{4,20},{20... | collective-permute-start | bytes 3145736 | tf_op jit(solution)/shard_map/ppermute | solution.py:105
  669.0 25.4 %collective-permute-start.106 = (bf16[704,512]{1,0:T(8,128)(2,1)S(1)}, bf16[704,512]{1,0:T(8,128)(2,1)S(1)}, u32[]{:S(2)}, u32[]{:S(2)}) collective-permute-start(bf16[704,512]{1,0:T(8,128)(2,1)S(1)} %concatenate.302), channel_id=1, source_target_pairs={{0,8},{4,12},{8,0},{12,4},{1,9},{5,13},{9,1},{13,5},{2,10},{6,14},... | collective-permute-start | bytes 2162696 | tf_op jit(solution)/shard_map/ppermute | solution.py:102
  694.4 49.6 %collective-permute-start.65 = (bf16[1024,1024]{1,0:T(8,128)(2,1)}, bf16[1024,1024]{1,0:T(8,128)(2,1)}, u32[]{:S(2)}, u32[]{:S(2)}) collective-permute-start(bf16[1024,1024]{1,0:T(8,128)(2,1)} %pad_maximum_fusion.3), channel_id=1, source_target_pairs={{0,16},{16,0},{1,17},{17,1},{2,18},{18,2},{3,19},{19,3},{4,20},{20... | collective-permute-start | bytes 6291464 | tf_op jit(solution)/shard_map/ppermute | solution.py:105
  707.8 49.2 %collective-permute-start.68 = (bf16[1024,1024]{1,0:T(8,128)(2,1)}, bf16[1024,1024]{1,0:T(8,128)(2,1)S(1)}, u32[]{:S(2)}, u32[]{:S(2)}) collective-permute-start(bf16[1024,1024]{1,0:T(8,128)(2,1)} %pad_maximum_fusion.4), channel_id=1, source_target_pairs={{0,16},{16,0},{1,17},{17,1},{2,18},{18,2},{3,19},{19,3},{4,20},{20... | collective-permute-start | bytes 6291464 | tf_op jit(solution)/shard_map/ppermute | solution.py:105
  708.4 41.1 %collective-permute-start.87 = (bf16[1024,1024]{0,1:T(8,128)(2,1)}, bf16[1024,1024]{0,1:T(8,128)(2,1)}, u32[]{:S(2)}, u32[]{:S(2)}) collective-permute-start(bf16[1024,1024]{0,1:T(8,128)(2,1)} %pad_maximum_fusion.5), channel_id=1, source_target_pairs={{0,16},{16,0},{1,17},{17,1},{2,18},{18,2},{3,19},{19,3},{4,20},{20... | collective-permute-start | bytes 6291464 | tf_op jit(solution)/shard_map/ppermute | solution.py:105
  710.0 27.8 %collective-permute-start.61 = (bf16[256,2048]{1,0:T(8,128)(2,1)}, bf16[256,2048]{1,0:T(8,128)(2,1)}, u32[]{:S(2)}, u32[]{:S(2)}) collective-permute-start(bf16[256,2048]{1,0:T(8,128)(2,1)} %fusion.43), channel_id=1, source_target_pairs={{0,1},{1,2},{2,3},{3,0},{4,5},{5,6},{6,7},{7,4},{8,9},{9,10},{10,1... | collective-permute-start | bytes 3145736 | tf_op jit(solution)/shard_map/ppermute | solution.py:108
  730.9 28.1 %collective-permute-start.90 = (bf16[1024,1024]{0,1:T(8,128)(2,1)}, bf16[1024,1024]{0,1:T(8,128)(2,1)S(1)}, u32[]{:S(2)}, u32[]{:S(2)}) collective-permute-start(bf16[1024,1024]{0,1:T(8,128)(2,1)} %pad_maximum_fusion.6), channel_id=1, source_target_pairs={{0,16},{16,0},{1,17},{17,1},{2,18},{18,2},{3,19},{19,3},{4,20},{20... | collective-permute-start | bytes 6291464 | tf_op jit(solution)/shard_map/ppermute | solution.py:105
  744.0 120.0 %collective-permute-start.97 = (bf16[512,1408]{1,0:T(8,128)(2,1)}, bf16[512,1408]{1,0:T(8,128)(2,1)}, u32[]{:S(2)}, u32[]{:S(2)}) collective-permute-start(bf16[512,1408]{1,0:T(8,128)(2,1)} %pad_maximum_fusion.8), channel_id=1, source_target_pairs={{0,4},{4,0},{8,12},{12,8},{1,5},{5,1},{9,13},{13,9},{2,6},{6,2},{1... | collective-permute-start | bytes 4325384 | tf_op jit(solution)/shard_map/ppermute | solution.py:102
  749.3 47.0 %collective-permute-start.62 = (bf16[256,2048]{1,0:T(8,128)(2,1)}, bf16[256,2048]{1,0:T(8,128)(2,1)}, u32[]{:S(2)}, u32[]{:S(2)}) collective-permute-start(bf16[256,2048]{1,0:T(8,128)(2,1)} %fusion.42), channel_id=1, source_target_pairs={{0,1},{1,2},{2,3},{3,0},{4,5},{5,6},{6,7},{7,4},{8,9},{9,10},{10,1... | collective-permute-start | bytes 3145736 | tf_op jit(solution)/shard_map/ppermute | solution.py:108
  749.4 33.7 %collective-permute-start.79 = (bf16[256,512]{1,0:T(8,128)(2,1)S(1)}, bf16[256,512]{1,0:T(8,128)(2,1)S(1)}, u32[]{:S(2)}, u32[]{:S(2)}) collective-permute-start(bf16[256,512]{1,0:T(8,128)(2,1)S(1)} %fusion.95), channel_id=1, source_target_pairs={{0,3},{1,2},{2,1},{3,0},{4,7},{5,6},{6,5},{7,4},{8,11},{9,10},{10,... | collective-permute-start | bytes 786440 | tf_op jit(solution)/shard_map/ppermute | solution.py:114
  757.1 37.3 %collective-permute-start.78 = (bf16[256,512]{1,0:T(8,128)(2,1)S(1)}, bf16[256,512]{1,0:T(8,128)(2,1)S(1)}, u32[]{:S(2)}, u32[]{:S(2)}) collective-permute-start(bf16[256,512]{1,0:T(8,128)(2,1)S(1)} %fusion.95), channel_id=1, source_target_pairs={{0,2},{1,3},{2,0},{3,1},{4,6},{5,7},{6,4},{7,5},{8,10},{9,11},{10,... | collective-permute-start | bytes 786440 | tf_op jit(solution)/shard_map/ppermute | solution.py:114
  759.1 35.6 %collective-permute-start.77 = (bf16[256,512]{1,0:T(8,128)(2,1)S(1)}, bf16[256,512]{1,0:T(8,128)(2,1)S(1)}, u32[]{:S(2)}, u32[]{:S(2)}) collective-permute-start(bf16[256,512]{1,0:T(8,128)(2,1)S(1)} %fusion.95), channel_id=1, source_target_pairs={{0,1},{1,0},{2,3},{3,2},{4,5},{5,4},{6,7},{7,6},{8,9},{9,8},{10,11... | collective-permute-start | bytes 786440 | tf_op jit(solution)/shard_map/ppermute | solution.py:114
  783.1 26.1 %collective-permute-start.66 = (bf16[512,1024]{1,0:T(8,128)(2,1)S(1)}, bf16[512,1024]{1,0:T(8,128)(2,1)S(1)}, u32[]{:S(2)}, u32[]{:S(2)}) collective-permute-start(bf16[512,1024]{1,0:T(8,128)(2,1)S(1)} %copy-done.120), channel_id=1, source_target_pairs={{0,8},{4,12},{8,0},{12,4},{1,9},{5,13},{9,1},{13,5},{2,10},{6,14},... | collective-permute-start | bytes 3145736 | tf_op jit(solution)/shard_map/ppermute | solution.py:102
  794.4 51.4 %collective-permute-start.69 = (bf16[512,1024]{1,0:T(8,128)(2,1)S(1)}, bf16[512,1024]{1,0:T(8,128)(2,1)S(1)}, u32[]{:S(2)}, u32[]{:S(2)}) collective-permute-start(bf16[512,1024]{1,0:T(8,128)(2,1)S(1)} %pad_maximum_fusion.22), channel_id=1, source_target_pairs={{0,4},{4,0},{8,12},{12,8},{1,5},{5,1},{9,13},{13,9},{2,6},{6,2},{1... | collective-permute-start | bytes 3145736 | tf_op jit(solution)/shard_map/ppermute | solution.py:102
  794.7 34.3 %collective-permute-start.88 = (bf16[1024,512]{0,1:T(8,128)(2,1)}, bf16[1024,512]{0,1:T(8,128)(2,1)S(1)}, u32[]{:S(2)}, u32[]{:S(2)}) collective-permute-start(bf16[1024,512]{0,1:T(8,128)(2,1)} %concatenate.300), channel_id=1, source_target_pairs={{0,8},{4,12},{8,0},{12,4},{1,9},{5,13},{9,1},{13,5},{2,10},{6,14},... | collective-permute-start | bytes 3145736 | tf_op jit(solution)/shard_map/ppermute | solution.py:102
  796.3 58.2 %collective-permute-start.91 = (bf16[1024,512]{0,1:T(8,128)(2,1)}, bf16[1024,512]{0,1:T(8,128)(2,1)S(1)}, u32[]{:S(2)}, u32[]{:S(2)}) collective-permute-start(bf16[1024,512]{0,1:T(8,128)(2,1)} %pad_maximum_fusion.24), channel_id=1, source_target_pairs={{0,4},{4,0},{8,12},{12,8},{1,5},{5,1},{9,13},{13,9},{2,6},{6,2},{1... | collective-permute-start | bytes 3145736 | tf_op jit(solution)/shard_map/ppermute | solution.py:102
  809.2 36.6 %collective-permute-start.80 = (bf16[256,512]{1,0:T(8,128)(2,1)S(1)}, bf16[256,512]{1,0:T(8,128)(2,1)S(1)}, u32[]{:S(2)}, u32[]{:S(2)}) collective-permute-start(bf16[256,512]{1,0:T(8,128)(2,1)S(1)} %add_convert_fusion.2), channel_id=1, source_target_pairs={{0,4},{4,0},{8,12},{12,8},{1,5},{5,1},{9,13},{13,9},{2,6},{6,2},{1... | collective-permute-start | bytes 786440 | tf_op jit(solution)/shard_map/ppermute | solution.py:102
  856.0 34.5 %collective-permute-start.100 = (bf16[512,1408]{1,0:T(8,128)(2,1)S(1)}, bf16[512,1408]{1,0:T(8,128)(2,1)S(1)}, u32[]{:S(2)}, u32[]{:S(2)}) collective-permute-start(bf16[512,1408]{1,0:T(8,128)(2,1)S(1)} %copy-done.107), channel_id=1, source_target_pairs={{0,8},{4,12},{8,0},{12,4},{1,9},{5,13},{9,1},{13,5},{2,10},{6,14},... | collective-permute-start | bytes 4325384 | tf_op jit(solution)/shard_map/ppermute | solution.py:102
  857.4 35.5 %collective-permute-start.67 = (bf16[256,1024]{1,0:T(8,128)(2,1)}, bf16[256,1024]{1,0:T(8,128)(2,1)S(1)}, u32[]{:S(2)}, u32[]{:S(2)}) collective-permute-start(bf16[256,1024]{1,0:T(8,128)(2,1)} %fusion.77), channel_id=1, source_target_pairs={{0,4},{4,0},{8,12},{12,8},{1,5},{5,1},{9,13},{13,9},{2,6},{6,2},{1... | collective-permute-start | bytes 1572872 | tf_op jit(solution)/shard_map/ppermute | solution.py:102
  857.8 43.9 %collective-permute-start.70 = (bf16[256,1024]{1,0:T(8,128)(2,1)}, bf16[256,1024]{1,0:T(8,128)(2,1)S(1)}, u32[]{:S(2)}, u32[]{:S(2)}) collective-permute-start(bf16[256,1024]{1,0:T(8,128)(2,1)} %fusion.74), channel_id=1, source_target_pairs={{0,8},{4,12},{8,0},{12,4},{1,9},{5,13},{9,1},{13,5},{2,10},{6,14},... | collective-permute-start | bytes 1572872 | tf_op jit(solution)/shard_map/ppermute | solution.py:102
  858.4 45.4 %collective-permute-start.89 = (bf16[1024,256]{0,1:T(8,128)(2,1)S(1)}, bf16[1024,256]{0,1:T(8,128)(2,1)S(1)}, u32[]{:S(2)}, u32[]{:S(2)}) collective-permute-start(bf16[1024,256]{0,1:T(8,128)(2,1)S(1)} %fusion.71), channel_id=1, source_target_pairs={{0,4},{4,0},{8,12},{12,8},{1,5},{5,1},{9,13},{13,9},{2,6},{6,2},{1... | collective-permute-start | bytes 1572872 | tf_op jit(solution)/shard_map/ppermute | solution.py:102
  864.0 49.0 %collective-permute-start.92 = (bf16[1024,256]{0,1:T(8,128)(2,1)S(1)}, bf16[1024,256]{0,1:T(8,128)(2,1)S(1)}, u32[]{:S(2)}, u32[]{:S(2)}) collective-permute-start(bf16[1024,256]{0,1:T(8,128)(2,1)S(1)} %copy-done.130), channel_id=1, source_target_pairs={{0,8},{4,12},{8,0},{12,4},{1,9},{5,13},{9,1},{13,5},{2,10},{6,14},... | collective-permute-start | bytes 1572872 | tf_op jit(solution)/shard_map/ppermute | solution.py:102
  890.5 57.0 %collective-permute-start.98 = (bf16[256,1408]{1,0:T(8,128)(2,1)S(1)}, bf16[256,1408]{1,0:T(8,128)(2,1)}, u32[]{:S(2)}, u32[]{:S(2)}) collective-permute-start(bf16[256,1408]{1,0:T(8,128)(2,1)S(1)} %fusion.59), channel_id=1, source_target_pairs={{0,8},{4,12},{8,0},{12,4},{1,9},{5,13},{9,1},{13,5},{2,10},{6,14},... | collective-permute-start | bytes 2162696 | tf_op jit(solution)/shard_map/ppermute | solution.py:102
  892.9 57.7 %collective-permute-start.101 = (bf16[256,1408]{1,0:T(8,128)(2,1)}, bf16[256,1408]{1,0:T(8,128)(2,1)}, u32[]{:S(2)}, u32[]{:S(2)}) collective-permute-start(bf16[256,1408]{1,0:T(8,128)(2,1)} %fusion.57), channel_id=1, source_target_pairs={{0,4},{4,0},{8,12},{12,8},{1,5},{5,1},{9,13},{13,9},{2,6},{6,2},{1... | collective-permute-start | bytes 2162696 | tf_op jit(solution)/shard_map/ppermute | solution.py:102
  903.8 30.3 %collective-permute-start.72 = (bf16[256,512]{1,0:T(8,128)(2,1)S(1)}, bf16[256,512]{1,0:T(8,128)(2,1)S(1)}, u32[]{:S(2)}, u32[]{:S(2)}) collective-permute-start(bf16[256,512]{1,0:T(8,128)(2,1)S(1)} %get-tuple-element.382), channel_id=1, source_target_pairs={{0,2},{1,3},{2,0},{3,1},{4,6},{5,7},{6,4},{7,5},{8,10},{9,11},{10,... | collective-permute-start | bytes 786440 | tf_op jit(solution)/shard_map/ppermute | solution.py:114
  913.0 21.1 %collective-permute-start.71 = (bf16[256,512]{1,0:T(8,128)(2,1)S(1)}, bf16[256,512]{1,0:T(8,128)(2,1)S(1)}, u32[]{:S(2)}, u32[]{:S(2)}) collective-permute-start(bf16[256,512]{1,0:T(8,128)(2,1)S(1)} %get-tuple-element.381), channel_id=1, source_target_pairs={{0,1},{1,0},{2,3},{3,2},{4,5},{5,4},{6,7},{7,6},{8,9},{9,8},{10,11... | collective-permute-start | bytes 786440 | tf_op jit(solution)/shard_map/ppermute | solution.py:114
  913.3 25.2 %collective-permute-start.95 = (bf16[512,256]{0,1:T(8,128)(2,1)S(1)}, bf16[512,256]{0,1:T(8,128)(2,1)S(1)}, u32[]{:S(2)}, u32[]{:S(2)}) collective-permute-start(bf16[512,256]{0,1:T(8,128)(2,1)S(1)} %get-tuple-element.372), channel_id=1, source_target_pairs={{0,3},{1,2},{2,1},{3,0},{4,7},{5,6},{6,5},{7,4},{8,11},{9,10},{10,... | collective-permute-start | bytes 786440 | tf_op jit(solution)/shard_map/ppermute | solution.py:114
  (227 other events, 2630.2 us)
